TPU v7x, 128 devices: a whole 4x4x4 slice. The times are simulated.
128 devices in a mesh: region: 16 (over x, z), sub: 8 (over y, core).
Axes of the slice: x: 4, y: 4, z: 4, core: 2. Of those that a mesh axis runs over, the one named last changes fastest.
Arguments:
- kkt_inverse: bfloat16 [262144, 2048], P(('region', 'sub')), may hold values from -0.125 to 0.125
- cost_terms: bfloat16 [262144, 256], P(('region', 'sub')), may hold values from -6 to 6
- dual_start: float32 [196608, 256], P(('region', 'sub')), may hold values from -4 to 4
- consensus_start: float32 [32768, 256], P(('region', 'sub')), may hold values from -6 to 6
- block_target: int32 [128, 12], P(('region', 'sub')), may hold values from -1 to 31, as said below
Outputs:
- state: float32 [262144, 256], P(('region', 'sub'))
- duals: float32 [196608, 256], P(('region', 'sub'))
- consensus: float32 [32768, 256], P(('region', 'sub'))
- norms: float32 [2, 2], replicated
Inputs may be any that keep to these rules, and one draw needn't show every extreme that they name: `block_target`: A device has at most 2 live blocks bound for one region, and every device has exactly 2 for some region. At least 10 of a device's slots are live; some device has all 12 live.
All inputs are finite; a program needn't handle non-finite values.
Results may differ from a plain program's by a relative error of at most 0.0034.
Values sent between devices are 32-bit elements; how exact they have to be, the bound alone decides.
A program may use at most 128 MiB of HBM per device.

v0:
```python
import jax
import jax.numpy as jnp
from jax import lax
from jax.sharding import Mesh
from jax.sharding import PartitionSpec as P

BLOCK = 128
CAP = 2
ITERS = 2
REGION = ("region_0", "region_1")
SUB = ("sub_0", "sub_1")
REGION_SUB = ("region_0", "region_1", "sub_0", "sub_1")


penalty = 1.5


def one_axis_at_a_time(shard, axes):
    for axis in axes:
        shard = lax.psum(shard, axis)
    return shard


def shards(kkt_inverse, cost_terms, dual_start, consensus_start, block_target):
    highest = lax.Precision.HIGHEST
    scen = cost_terms.shape[1]
    target = block_target[0]
    blocks = target.shape[0]
    bound_rows = blocks * BLOCK
    owned = consensus_start.shape[0] // BLOCK
    peers = lax.axis_size(REGION)
    devices = peers * lax.axis_size(SUB)
    live = target >= 0
    livef = live.astype(jnp.float32)
    base = jnp.dot(kkt_inverse, cost_terms, preferred_element_type=jnp.float32)
    coupling = kkt_inverse[:, :bound_rows]
    dual = dual_start.reshape(blocks, BLOCK * scen)
    cons = consensus_start.reshape(owned, BLOCK * scen)
    peer = jnp.where(live, target // owned, -1)
    same = (peer[:, None] == peer[None, :]) & live[:, None]
    earlier = jnp.arange(blocks)[:, None] < jnp.arange(blocks)[None, :]
    rank = jnp.sum((same & earlier).astype(jnp.int32), axis=0)
    slot = jnp.where(live, peer * CAP + rank, -1)
    match = slot[None, :] == jnp.arange(peers * CAP, dtype=jnp.int32)[:, None]
    send_hot = match.astype(jnp.float32)
    labels = jnp.max(jnp.where(match, (target % owned)[None, :], -1), axis=1)
    got_labels = lax.all_to_all(
        labels.reshape(peers, CAP), REGION, split_axis=0, concat_axis=0, tiled=True
    ).reshape(peers * CAP)
    recv_hot = (got_labels[None, :] == jnp.arange(owned, dtype=jnp.int32)[:, None]).astype(
        jnp.float32
    )
    counts = jnp.sum(recv_hot, axis=1)

    def fetch(values):
        reply = jnp.dot(recv_hot.T, values, precision=highest).reshape(peers, CAP, -1)
        back = lax.all_to_all(reply, REGION, split_axis=0, concat_axis=0, tiled=True).reshape(
            peers * CAP, -1
        )
        return jnp.dot(send_hot.T, back, precision=highest)

    floor_counts = jnp.maximum(counts, 1.0)
    fetched = fetch(cons)
    field = base
    rows = []
    for step in range(ITERS):
        drive = (
            (penalty * livef[:, None] * (fetched - dual))
            .reshape(bound_rows, scen)
            .astype(jnp.bfloat16)
        )
        field = base + jnp.dot(coupling, drive, preferred_element_type=jnp.float32)
        copies = field[:bound_rows].reshape(blocks, BLOCK * scen)
        outgoing = jnp.dot(send_hot, copies + dual, precision=highest).reshape(peers, CAP, -1)
        incoming = lax.all_to_all(
            outgoing, REGION, split_axis=0, concat_axis=0, tiled=True
        ).reshape(peers * CAP, -1)
        sums = jnp.dot(recv_hot, incoming, precision=highest)
        renewed = sums / floor_counts[:, None]
        fetched = fetch(renewed)
        gap = copies - fetched
        primal = jnp.sum(livef[:, None] * gap * gap)
        change = renewed - cons
        moved = penalty * penalty * jnp.sum(counts[:, None] * change * change)
        dual = dual + livef[:, None] * gap
        cons = renewed
        rows.append(jnp.stack([primal, moved]))
    table = jnp.stack(rows)
    table = one_axis_at_a_time(table, REGION_SUB)
    norms = jnp.sqrt(table / (devices * scen * BLOCK))
    return (field, dual.reshape(bound_rows, scen), cons.reshape(owned * BLOCK, scen), norms)


def solution(mesh):
    split = Mesh(mesh.devices.reshape(4, 4, 4, 2), ("region_0", "region_1", "sub_0", "sub_1"))
    return jax.shard_map(
        shards,
        mesh=split,
        in_specs=(
            P(REGION_SUB, None),
            P(REGION_SUB, None),
            P(REGION_SUB, None),
            P(REGION_SUB, None),
            P(REGION_SUB, None),
        ),
        out_specs=(P(REGION_SUB, None), P(REGION_SUB, None), P(REGION_SUB, None), P()),
        check_vma=False,
    )
```

profile of v0, /device:TPU:1, one launch (start us, length us, event | category | flops | bytes accessed | tf_op | source)
XLA Modules:
  0.0 468.6 jit_solution(12082405506811106213)
XLA Ops:
  4.3 8.4 %all-to-all-start = ((s32[16,1,2]{2,1,0:T(1,128)}), s32[16,1,2]{2,1,0:T(1,128)S(1)}, u32[]{:S(2)}, u32[]{:S(2)}) async-start(s32[16,1,2]{2,1,0:T(1,128)} %bitcast.5), calls=%async_computation | async-start | bytes 16384 | tf_op jit(solution)/shard_map/all_to_all | solution.py:47
  13.8 5.2 %all-to-all-done = s32[16,1,2]{2,1,0:T(1,128)S(1)} async-done(((s32[16,1,2]{2,1,0:T(1,128)}), s32[16,1,2]{2,1,0:T(1,128)S(1)}, u32[]{:S(2)}, u32[]{:S(2)}) %all-to-all-start) | async-done | bytes 160 | tf_op jit(solution)/shard_map/all_to_all | solution.py:47
  21.2 5.2 %copy.25 = f32[16,2,32768]{2,1,0:T(2,128)} copy(f32[16,2,32768]{2,0,1:T(8,128)S(1)} %fusion.31) | data formatting | bytes 8388608 | tf_op jit(solution)/shard_map/dot_general | solution.py:56
  26.4 5.1 %all-to-all-start.1 = ((f32[16,2,32768]{2,1,0:T(2,128)}), f32[16,2,32768]{2,1,0:T(2,128)}, u32[]{:S(2)}, u32[]{:S(2)}) async-start(f32[16,2,32768]{2,1,0:T(2,128)} %copy.25), calls=%async_computation.1 | async-start | bytes 8388608 | tf_op jit(solution)/shard_map/all_to_all | solution.py:57
  33.2 7.8 %fusion.47 = f32[2048,256]{1,0:T(8,128)} fusion(bf16[2048,2048]{1,0:T(8,128)(2,1)} %param.5, bf16[2048,256]{1,0:T(8,128)(2,1)S(1)} %copy-done), kind=kOutput, calls=%fused_computation.80 | convolution fusion | flops 2147483648 | bytes 11534336 | tf_op jit(solution)/shard_map/dot_general | solution.py:35
  41.0 42.3 %all-to-all-done.1 = f32[16,2,32768]{2,1,0:T(2,128)} async-done(((f32[16,2,32768]{2,1,0:T(2,128)}), f32[16,2,32768]{2,1,0:T(2,128)}, u32[]{:S(2)}, u32[]{:S(2)}) %all-to-all-start.1) | async-done | bytes 4194336 | tf_op jit(solution)/shard_map/all_to_all | solution.py:57
  83.3 6.0 %reshape.150 = f32[32,32768]{1,0:T(8,128)} reshape(f32[16,2,32768]{2,1,0:T(2,128)} %all-to-all-done.1) | data formatting | bytes 8388608 | tf_op jit(solution)/shard_map/reshape | solution.py:57
  94.0 4.8 %fusion.9 = f32[2048,256]{1,0:T(8,128)S(1)} fusion(bf16[1536,256]{1,0:T(8,128)(2,1)S(1)} %convert_element_type.29, bf16[2048,2048]{1,0:T(8,128)(2,1)} %param.5), kind=kOutput, calls=%fused_computation.15 | convolution fusion | flops 1610612736 | bytes 9175040 | tf_op jit(solution)/shard_map/dot_general | solution.py:72
  104.5 5.2 %copy.27 = f32[16,2,32768]{2,1,0:T(2,128)} copy(f32[16,2,32768]{2,0,1:T(8,128)S(1)} %fusion.21) | data formatting | bytes 8388608 | tf_op jit(solution)/shard_map/dot_general | solution.py:74
  109.7 5.6 %all-to-all-start.2 = ((f32[16,2,32768]{2,1,0:T(2,128)}), f32[16,2,32768]{2,1,0:T(2,128)}, u32[]{:S(2)}, u32[]{:S(2)}) async-start(f32[16,2,32768]{2,1,0:T(2,128)} %copy.27), calls=%async_computation.2 | async-start | bytes 8388608 | tf_op jit(solution)/shard_map/all_to_all | solution.py:75
  116.7 45.7 %all-to-all-done.2 = f32[16,2,32768]{2,1,0:T(2,128)} async-done(((f32[16,2,32768]{2,1,0:T(2,128)}), f32[16,2,32768]{2,1,0:T(2,128)}, u32[]{:S(2)}, u32[]{:S(2)}) %all-to-all-start.2) | async-done | bytes 4194336 | tf_op jit(solution)/shard_map/all_to_all | solution.py:75
  162.4 6.0 %reshape.152 = f32[32,32768]{1,0:T(8,128)} reshape(f32[16,2,32768]{2,1,0:T(2,128)} %all-to-all-done.2) | data formatting | bytes 8388608 | tf_op jit(solution)/shard_map/reshape | solution.py:77
  175.6 5.8 %reshape.153 = f32[16,2,32768]{2,1,0:T(2,128)} reshape(f32[32,32768]{1,0:T(8,128)} %fusion.37) | data formatting | bytes 8388608 | tf_op jit(solution)/shard_map/reshape | solution.py:56
  181.4 10.5 %all-to-all-start.3 = ((f32[16,2,32768]{2,1,0:T(2,128)}), f32[16,2,32768]{2,1,0:T(2,128)}, u32[]{:S(2)}, u32[]{:S(2)}) async-start(f32[16,2,32768]{2,1,0:T(2,128)} %reshape.153), calls=%async_computation.3 | async-start | bytes 8388608 | tf_op jit(solution)/shard_map/all_to_all | solution.py:57
  193.6 45.0 %all-to-all-done.3 = f32[16,2,32768]{2,1,0:T(2,128)} async-done(((f32[16,2,32768]{2,1,0:T(2,128)}), f32[16,2,32768]{2,1,0:T(2,128)}, u32[]{:S(2)}, u32[]{:S(2)}) %all-to-all-start.3) | async-done | bytes 4194336 | tf_op jit(solution)/shard_map/all_to_all | solution.py:57
  238.5 6.1 %reshape.154 = f32[32,32768]{1,0:T(8,128)} reshape(f32[16,2,32768]{2,1,0:T(2,128)} %all-to-all-done.3) | data formatting | bytes 8388608 | tf_op jit(solution)/shard_map/reshape | solution.py:57
  244.6 6.9 %multiply_convert_fusion = (bf16[12,32768]{1,0:T(8,128)(2,1)S(1)}, f32[12,32768]{1,0:T(8,128)}, f32[12,32768]{1,0:T(8,128)}) fusion(f32[12]{0:T(128)S(1)} %broadcast_select_fusion, f32[12,32768]{1,0:T(8,128)} %copy-done.2, f32[12,32768]{1,0:T(8,128)S(1)} %reshape.155, f32[12]{0:T(128)S(1)} %get-tuple-element.13, f32[32,32768]{1,0:T(8,128)} %reshape.154, ...), kind=kOutput, calls=%fused_computation.21 | convolution fusion | flops 153354624 | bytes 11272336 | tf_op jit(solution)/shard_map/dot_general | solution.py:60
  252.8 5.4 %fusion.12 = f32[2048,256]{1,0:T(8,128)S(1)} fusion(f32[2048,256]{1,0:T(8,128)} %fusion.47, bf16[1536,256]{1,0:T(8,128)(2,1)} %convert_element_type.33, bf16[2048,2048]{1,0:T(8,128)(2,1)} %param.5), kind=kOutput, calls=%fused_computation.16 | convolution fusion | flops 1611137024 | bytes 11272192 | tf_op jit(solution)/shard_map/dot_general | solution.py:72
  263.6 6.1 %fusion.17 = f32[32,32768]{1,0:T(8,128)} fusion(f32[12,32768]{1,0:T(8,128)} %reshape.156, f32[12,32768]{1,0:T(8,128)} %get-tuple-element.9, s32[12]{0:T(128)S(1)} %get-tuple-element.15), kind=kOutput, calls=%fused_computation.19 | convolution fusion | flops 151388544 | bytes 7340080 | tf_op jit(solution)/shard_map/dot_general | solution.py:74
  269.7 5.8 %reshape.157 = f32[16,2,32768]{2,1,0:T(2,128)} reshape(f32[32,32768]{1,0:T(8,128)} %fusion.17) | data formatting | bytes 8388608 | tf_op jit(solution)/shard_map/reshape | solution.py:74
  275.5 10.1 %all-to-all-start.4 = ((f32[16,2,32768]{2,1,0:T(2,128)}), f32[16,2,32768]{2,1,0:T(2,128)}, u32[]{:S(2)}, u32[]{:S(2)}) async-start(f32[16,2,32768]{2,1,0:T(2,128)} %reshape.157), calls=%async_computation.4 | async-start | bytes 8388608 | tf_op jit(solution)/shard_map/all_to_all | solution.py:75
  285.9 46.7 %all-to-all-done.4 = f32[16,2,32768]{2,1,0:T(2,128)} async-done(((f32[16,2,32768]{2,1,0:T(2,128)}), f32[16,2,32768]{2,1,0:T(2,128)}, u32[]{:S(2)}, u32[]{:S(2)}) %all-to-all-start.4) | async-done | bytes 4194336 | tf_op jit(solution)/shard_map/all_to_all | solution.py:75
  332.5 6.0 %reshape.158 = f32[32,32768]{1,0:T(8,128)} reshape(f32[16,2,32768]{2,1,0:T(2,128)} %all-to-all-done.4) | data formatting | bytes 8388608 | tf_op jit(solution)/shard_map/reshape | solution.py:77
  346.4 5.8 %reshape.159 = f32[16,2,32768]{2,1,0:T(2,128)} reshape(f32[32,32768]{1,0:T(8,128)} %fusion.36) | data formatting | bytes 8388608 | tf_op jit(solution)/shard_map/reshape | solution.py:56
  352.3 10.5 %all-to-all-start.5 = ((f32[16,2,32768]{2,1,0:T(2,128)}), f32[16,2,32768]{2,1,0:T(2,128)}, u32[]{:S(2)}, u32[]{:S(2)}) async-start(f32[16,2,32768]{2,1,0:T(2,128)} %reshape.159), calls=%async_computation.5 | async-start | bytes 8388608 | tf_op jit(solution)/shard_map/all_to_all | solution.py:57
  364.1 45.7 %all-to-all-done.5 = f32[16,2,32768]{2,1,0:T(2,128)} async-done(((f32[16,2,32768]{2,1,0:T(2,128)}), f32[16,2,32768]{2,1,0:T(2,128)}, u32[]{:S(2)}, u32[]{:S(2)}) %all-to-all-start.5) | async-done | bytes 4194336 | tf_op jit(solution)/shard_map/all_to_all | solution.py:57
  409.7 6.1 %reshape.160 = f32[32,32768]{1,0:T(8,128)} reshape(f32[16,2,32768]{2,1,0:T(2,128)} %all-to-all-done.5) | data formatting | bytes 8388608 | tf_op jit(solution)/shard_map/reshape | solution.py:57
  415.8 8.4 %fusion.15 = (f32[]{:T(128)}, f32[]{:T(128)}, f32[12,32768]{1,0:T(8,128)}) fusion(f32[12]{0:T(128)S(1)} %get-tuple-element.13, f32[12,32768]{1,0:T(8,128)S(1)} %reshape.155, f32[12,32768]{1,0:T(8,128)} %get-tuple-element.17, f32[12,32768]{1,0:T(8,128)} %get-tuple-element.9, f32[12,32768]{1,0:T(8,128)} %reshape.156, f32[32,32768]{1,0:T(8,128)} %reshape.160, ...), kind=kOutput, calls=%fused_computation.17 | convolution fusion | flops 154534272 | bytes 12058728 | tf_op jit(solution)/shard_map/dot_general | solution.py:60
  425.5 9.0 %psum.28 = f32[2,2]{1,0:T(2,128)S(1)} all-reduce(f32[2,2]{1,0:T(2,128)S(1)} %pad_maximum_fusion), channel_id=1, replica_groups=mesh['region_0'=4,'region_1'=4,'sub_0'=4,'sub_1'=2] {'region_0'}, use_global_device_ids=true, to_apply=%region_7.8 | all-reduce | flops 4 | bytes 32 | tf_op jit(solution)/shard_map/psum | solution.py:20
  434.5 11.2 %psum.29 = f32[2,2]{1,0:T(2,128)S(1)} all-reduce(f32[2,2]{1,0:T(2,128)S(1)} %psum.28), channel_id=1, replica_groups=mesh['region_0'=4,'region_1'=4,'sub_0'=4,'sub_1'=2] {'region_1'}, use_global_device_ids=true, to_apply=%region_8.9 | all-reduce | flops 4 | bytes 32 | tf_op jit(solution)/shard_map/psum | solution.py:20
  445.7 8.9 %psum.30 = f32[2,2]{1,0:T(2,128)S(1)} all-reduce(f32[2,2]{1,0:T(2,128)S(1)} %psum.29), channel_id=1, replica_groups=mesh['region_0'=4,'region_1'=4,'sub_0'=4,'sub_1'=2] {'sub_0'}, use_global_device_ids=true, to_apply=%region_9.10 | all-reduce | flops 4 | bytes 32 | tf_op jit(solution)/shard_map/psum | solution.py:20
  455.5 9.6 %psum.31 = f32[2,2]{1,0:T(2,128)S(1)} all-reduce(f32[2,2]{1,0:T(2,128)S(1)} %psum.30), channel_id=1, replica_groups=mesh['region_0'=4,'region_1'=4,'sub_0'=4,'sub_1'=2] {'sub_1'}, use_global_device_ids=true, to_apply=%region_10.11 | all-reduce | flops 4 | bytes 32 | tf_op jit(solution)/shard_map/psum | solution.py:20
  (57 shorter events, 49.3 us)
Async XLA Ops:
  0.6 32.6 %copy-start = (bf16[2048,256]{1,0:T(8,128)(2,1)S(1)}, bf16[2048,256]{1,0:T(8,128)(2,1)}, u32[]{:S(2)}) copy-start(bf16[2048,256]{1,0:T(8,128)(2,1)} %param.6) | copy-start | bytes 3145732
  4.3 14.8 %all-to-all-start = ((s32[16,1,2]{2,1,0:T(1,128)}), s32[16,1,2]{2,1,0:T(1,128)S(1)}, u32[]{:S(2)}, u32[]{:S(2)}) async-start(s32[16,1,2]{2,1,0:T(1,128)} %bitcast.5), calls=%async_computation | async-start | bytes 16384 | tf_op jit(solution)/shard_map/all_to_all | solution.py:47
  26.4 56.8 %all-to-all-start.1 = ((f32[16,2,32768]{2,1,0:T(2,128)}), f32[16,2,32768]{2,1,0:T(2,128)}, u32[]{:S(2)}, u32[]{:S(2)}) async-start(f32[16,2,32768]{2,1,0:T(2,128)} %copy.25), calls=%async_computation.1 | async-start | bytes 8388608 | tf_op jit(solution)/shard_map/all_to_all | solution.py:57
  31.5 1.7 copy-start.9
  33.2 56.1 %copy-start.2 = (f32[12,32768]{1,0:T(8,128)}, f32[12,32768]{1,0:T(8,128)S(1)}, u32[]{:S(2)}) copy-start(f32[12,32768]{1,0:T(8,128)S(1)} %reshape.151) | copy-start | bytes 4718596
  94.0 4.8 %copy-start.3 = (f32[1536,256]{1,0:T(8,128)S(1)}, f32[1536,256]{1,0:T(8,128)}, u32[]{:S(2)}) copy-start(f32[1536,256]{1,0:T(8,128)} %param.7) | copy-start | bytes 4718596
  94.0 4.8 %copy-start.5 = (f32[2048,256]{1,0:T(8,128)S(1)}, f32[2048,256]{1,0:T(8,128)}, u32[]{:S(2)}) copy-start(f32[2048,256]{1,0:T(8,128)} %fusion.47) | copy-start | bytes 6291460
  109.7 52.7 %all-to-all-start.2 = ((f32[16,2,32768]{2,1,0:T(2,128)}), f32[16,2,32768]{2,1,0:T(2,128)}, u32[]{:S(2)}, u32[]{:S(2)}) async-start(f32[16,2,32768]{2,1,0:T(2,128)} %copy.27), calls=%async_computation.2 | async-start | bytes 8388608 | tf_op jit(solution)/shard_map/all_to_all | solution.py:75
  181.4 57.2 %all-to-all-start.3 = ((f32[16,2,32768]{2,1,0:T(2,128)}), f32[16,2,32768]{2,1,0:T(2,128)}, u32[]{:S(2)}, u32[]{:S(2)}) async-start(f32[16,2,32768]{2,1,0:T(2,128)} %reshape.153), calls=%async_computation.3 | async-start | bytes 8388608 | tf_op jit(solution)/shard_map/all_to_all | solution.py:57
  258.3 1.3 copy-start.4
  275.5 10.2 %copy-start.8 = (f32[256,256]{1,0:T(8,128)S(1)}, f32[256,256]{1,0:T(8,128)}, u32[]{:S(2)}) copy-start(f32[256,256]{1,0:T(8,128)} %param.8) | copy-start | bytes 786436
  275.5 57.0 %all-to-all-start.4 = ((f32[16,2,32768]{2,1,0:T(2,128)}), f32[16,2,32768]{2,1,0:T(2,128)}, u32[]{:S(2)}, u32[]{:S(2)}) async-start(f32[16,2,32768]{2,1,0:T(2,128)} %reshape.157), calls=%async_computation.4 | async-start | bytes 8388608 | tf_op jit(solution)/shard_map/all_to_all | solution.py:75
  343.0 3.4 copy-start.6
  352.3 57.4 %all-to-all-start.5 = ((f32[16,2,32768]{2,1,0:T(2,128)}), f32[16,2,32768]{2,1,0:T(2,128)}, u32[]{:S(2)}, u32[]{:S(2)}) async-start(f32[16,2,32768]{2,1,0:T(2,128)} %reshape.159), calls=%async_computation.5 | async-start | bytes 8388608 | tf_op jit(solution)/shard_map/all_to_all | solution.py:57
  415.8 38.8 %copy-start.7 = (f32[2,32768]{1,0:T(2,128)S(1)}, f32[2,32768]{1,0:T(2,128)}, u32[]{:S(2)}) copy-start(f32[2,32768]{1,0:T(2,128)} %copy-done.6) | copy-start | bytes 786436
  445.6 22.7 %copy-start.1 = (bf16[2048,256]{1,0:T(8,128)(2,1)S(1)}, bf16[2048,256]{1,0:T(8,128)(2,1)}, u32[]{:S(2)}) copy-start(bf16[2048,256]{1,0:T(8,128)(2,1)} %param.6) | copy-start | bytes 3145732
where the time goes:
time: 475 us; the launch traced here: 469 us
  waiting for transfers between devices  230 us (48%)
  local copies, waits for them, and re-layouts  76.9 us (16%)
  matrix products  62.2 us (13%)
  starting transfers between devices  50.2 us (11%)
  blocking collectives  38.7 us (8%)
  other arithmetic  7.64 us (2%)
    all_to_all x3, waiting for transfers between devices, fetch(): lax.all_to_all(reply, REGION, split_axis=0, concat_axis=0, tiled=True)  133 us
    all_to_all x2, waiting for transfers between devices, shards(): lax.all_to_all(outgoing, REGION, split_axis=0, concat_axis=0, tiled=True)  92.4 us
    psum x4, blocking collectives, one_axis_at_a_time(): shard = lax.psum(shard, axis)  38.7 us
    all_to_all x3, starting transfers between devices, fetch(): lax.all_to_all(reply, REGION, split_axis=0, concat_axis=0, tiled=True)  26.1 us
    dot_general x3, matrix products, fetch(): return jnp.dot(send_hot.T, back, precision=highest)  19.2 us
    reshape x3, local copies, waits for them, and re-layouts, fetch(): lax.all_to_all(reply, REGION, split_axis=0, concat_axis=0, tiled=True)  18.2 us
    all_to_all x2, starting transfers between devices, shards(): lax.all_to_all(outgoing, REGION, split_axis=0, concat_axis=0, tiled=True)  15.8 us
    reshape x2, local copies, waits for them, and re-layouts, shards(): incoming = lax.all_to_all(outgoing, REGION, split_axis=0, concat_axis=0,...  12.1 us
  transfers between devices with their start and end apart: 6, of which 6 were waited for; matrix products, arithmetic and copies ran while one was open for 3% of the time, Pallas kernels for 0%

commit v1 on v0

v1 whole, which is shorter than its diff:
```python
import functools

import jax
import jax.numpy as jnp
from jax import lax
from jax.experimental import pallas as pl
from jax.experimental.pallas import tpu as pltpu
from jax.sharding import PartitionSpec as P

MESH = pl.DeviceIdType.MESH
BLOCK = 128
ITERS = 2
RING = 4
ROWS = 16
LANES = 128
penalty = 1.5


def ring_add(a, e):
    return lax.rem(a + e, RING)


def kernel(
    kkt_ref, cost_ref, dual_ref, cons_ref, target_ref,
    state_ref, duals_ref, consensus_ref, norms_ref,
    kkt, cost, base, state, dual, cons, drive, tables, table_s, count_v, count_s, part, totals_a, totals_b,
    *rest,
):
    nb = target_ref.shape[1]
    owned = cons_ref.shape[0]
    n_region = RING * RING
    n_sub = lax.axis_size("sub")
    n_pos = n_region * owned
    mine = RING * owned
    bound = nb * BLOCK
    order = rest[0].shape[0]
    streams = [(c, h) for c in range(2) for h in range(2)]
    bufs = {}
    names = ("send", "got", "psum", "got2", "grid", "back", "fetched", "own")
    rest = list(rest)
    for s in streams:
        for name in names:
            bufs[name, s] = rest.pop(0)
    sem_local, sem_table, sem_init, sem_v, sem_p, sem_q, sem_w, sem_o, sem_n = rest
    del order

    r = lax.axis_index("region")
    sub = lax.axis_index("sub")
    x = r // RING
    z = lax.rem(r, RING)

    def first(h, e):
        return ring_add(x, e) * RING + z if h == 0 else x * RING + ring_add(z, e)

    def second(h, e):
        return first(1 - h, e)

    c1 = (x, z)
    c2 = (z, x)

    def remote(src, dst, sems, index, region):
        return pltpu.make_async_remote_copy(
            src_ref=src, dst_ref=dst, send_sem=sems.at[(0, *index)], recv_sem=sems.at[(1, *index)],
            device_id={"region": region}, device_id_type=MESH,
        )

    local = [
        pltpu.make_async_copy(cons_ref, cons, sem_local.at[0]),
        pltpu.make_async_copy(cost_ref, cost, sem_local.at[1]),
        pltpu.make_async_copy(dual_ref, dual, sem_local.at[2]),
        pltpu.make_async_copy(kkt_ref, kkt, sem_local.at[3]),
    ]
    for copy in local:
        copy.start()

    barrier = pltpu.get_barrier_semaphore()
    for e in range(1, n_region):
        pl.semaphore_signal(
            barrier, inc=1, device_id={"region": lax.rem(r + e, n_region)}, device_id_type=MESH
        )
    for e in range(1, n_sub):
        pl.semaphore_signal(barrier, inc=1, device_id={"sub": lax.rem(sub + e, n_sub)}, device_id_type=MESH)

    lane = lax.broadcasted_iota(jnp.int32, (8, LANES), 1)
    row = lax.broadcasted_iota(jnp.int32, (8, LANES), 0)
    none = jnp.full((8, LANES), nb, jnp.int32)
    one_a, one_b, two_a, two_b = none, none, none, none
    places = jnp.full((8, LANES), n_pos, jnp.int32)
    for s in range(nb):
        t = target_ref[0, s]
        pos_b = t
        pos_a = lax.rem(t // owned, RING) * mine + (t // (owned * RING)) * owned + lax.rem(t, owned)
        pos_a = jnp.where(t >= 0, pos_a, -1)
        hit_a = lane == pos_a
        hit_b = lane == pos_b
        two_a = jnp.where(hit_a & (one_a < nb), s, two_a)
        one_a = jnp.where(hit_a & (one_a == nb), s, one_a)
        two_b = jnp.where(hit_b & (one_b < nb), s, two_b)
        one_b = jnp.where(hit_b & (one_b == nb), s, one_b)
        here = jnp.where(row == 4, pos_a, pos_b)
        places = jnp.where((lane == s) & (t >= 0), here, places)
    tile = jnp.where(row == 0, one_a, places)
    tile = jnp.where(row == 1, two_a, tile)
    tile = jnp.where(row == 2, one_b, tile)
    tile = jnp.where(row == 3, two_b, tile)
    tables[pl.ds(r, 1)] = tile[None]

    zero = jnp.zeros((ROWS, LANES), jnp.float32)
    for s in streams:
        for p in range(RING):
            bufs["send", s][p, nb] = zero
        for p in range(RING - 1):
            bufs["got", s][p, nb] = zero
        bufs["grid", s][n_pos] = zero

    local[0].wait()
    pl.semaphore_wait(barrier, n_region - 1 + n_sub - 1)

    init = {}
    for s in streams:
        c, h = s
        for e in range(1, RING):
            p = ring_add(c1[h], e)
            at = pl.multiple_of(c2[h] * mine + c1[h] * owned, owned)
            src = cons.at[:, pl.ds(pl.multiple_of(h * RING * ROWS + p * ROWS, ROWS), ROWS), pl.ds(c * LANES, LANES)]
            init[s, e] = remote(src, bufs["grid", s].at[pl.ds(at, owned)], sem_init, (c, h, e - 1), first(h, e))
            init[s, e].start()
    table_copies = []
    for e in range(1, n_region):
        copy = remote(tables.at[r], tables.at[r], sem_table, (e - 1,), lax.rem(r + e, n_region))
        copy.start()
        table_copies.append(copy)
    for s in streams:
        c, h = s
        for o in range(owned):
            rows = pl.ds(pl.multiple_of(h * RING * ROWS + c1[h] * ROWS, ROWS), ROWS)
            bufs["grid", s][c2[h] * mine + c1[h] * owned + o] = cons[o, rows, c * LANES : (c + 1) * LANES]

    def send_grid(s):
        c, h = s
        copies = []
        at = pl.ds(pl.multiple_of(c2[h] * mine, mine), mine)
        for e in range(1, RING):
            copy = remote(
                bufs["grid", s].at[at], bufs["grid", s].at[at], sem_q, (c, h, e - 1), second(h, e)
            )
            copy.start()
            copies.append(copy)
        return copies

    q_copies, w_copies, v_copies, p_copies = {}, {}, {}, {}
    for s in streams:
        for e in range(1, RING):
            init[s, e].wait()
        q_copies[s] = send_grid(s)

    for copy in table_copies:
        copy.wait()
    peers = [r] + [first(0, e) for e in range(1, RING)] + [first(1, e) for e in range(1, RING)]
    moves = [
        pltpu.make_async_copy(tables.at[peer], table_s.at[i], sem_local.at[4 + i]) for i, peer in enumerate(peers)
    ]
    for move in moves:
        move.start()
    every = tables[...]
    used = jnp.sum((every < nb).astype(jnp.int32), axis=0).astype(jnp.float32)
    count_a = used[0:1] + used[1:2]
    count_b = used[2:3] + used[3:4]
    count_v[...] = jnp.where(row == 0, count_a, count_b)
    counting = pltpu.make_async_copy(count_v, count_s, sem_local.at[11])
    counting.start()
    for move in moves:
        move.wait()
    counting.wait()

    def table_of(h, e):
        return 0 if e == 0 else (e if h == 0 else RING - 1 + e)

    def live(s):
        return jnp.where(target_ref[0, s] >= 0, 1.0, 0.0).astype(jnp.float32)

    local[1].wait()
    local[3].wait()

    half = 256

    def base_rows(i, _):
        at = pl.ds(pl.multiple_of(i * half, half), half)
        base[at] = jnp.dot(kkt[at], cost[...], preferred_element_type=jnp.float32)
        return 0

    lax.fori_loop(0, kkt.shape[0] // half, base_rows, 0)
    local[2].wait()

    def gather_send(s, before):
        c, h = s
        for copy in q_copies[s]:
            copy.wait_recv()
        for copy in before:
            copy.wait_send()
        copies = []
        grid = bufs["grid", s]
        for e in (1, 3, 2, 0):
            t = table_of(h, e)

            def one(slot, _):
                value = grid[table_s[t, 4 + h, slot]]
                if e:
                    bufs["back", s][e - 1, slot] = value
                else:
                    bufs["own", s][slot] = value
                return 0

            lax.fori_loop(0, nb, one, 0, unroll=4)
            if e:
                copy = remote(
                    bufs["back", s].at[e - 1], bufs["fetched", s].at[e - 1], sem_w, (c, h, e - 1), first(h, e)
                )
                copy.start()
                copies.append(copy)
        return copies

    def fetched_rows(s, slot, p):
        c, h = s
        return bufs["fetched", s][lax.rem(c1[h] - p + RING, RING), slot]

    def own_into_place(s):
        pass

    part_primal = {}

    def update(c, step):
        cols = pl.ds(c * LANES, LANES)

        def one(slot, total):
            alive = live(slot)
            for h in range(2):
                s = (c, h)
                for e in range(RING):
                    p = lax.rem(c1[h] - e + RING, RING)
                    value = bufs["own", s][slot] if e == 0 else bufs["fetched", s][e - 1, slot]
                    in_block = pl.ds(pl.multiple_of(h * RING * ROWS + p * ROWS, ROWS), ROWS)
                    old = dual[slot, in_block, cols]
                    at = pl.ds(pl.multiple_of(slot * BLOCK + h * RING * ROWS + p * ROWS, ROWS), ROWS)
                    if step > 0:
                        gap = state[at, cols] - value
                        total = total + alive * gap * gap
                        old = old + alive * gap
                        dual[slot, in_block, cols] = old
                    if step < ITERS:
                        drive[at, cols] = (penalty * alive * (value - old)).astype(jnp.bfloat16)
            return total

        return lax.fori_loop(0, nb, one, jnp.zeros((ROWS, LANES), jnp.float32))

    slots_at_once = 4
    chunk = slots_at_once * BLOCK

    def couple_send(c, step):
        cols = pl.ds(c * LANES, LANES)
        for h in range(2):
            for copy in v_copies.get((c, h), ()):
                copy.wait_send()

        def one(i, _):
            at = pl.ds(pl.multiple_of(i * chunk, chunk), chunk)
            rows = base[at, cols] + jnp.dot(
                kkt[at, 0:bound], drive[:, cols], preferred_element_type=jnp.float32
            )
            state[at, cols] = rows
            for j in range(slots_at_once):
                slot = i * slots_at_once + j
                v = rows[j * BLOCK : (j + 1) * BLOCK] + dual[slot, :, cols]
                for h in range(2):
                    for p in range(RING):
                        lo = h * RING * ROWS + p * ROWS
                        bufs["send", (c, h)][p, slot] = v[lo : lo + ROWS]
            return 0

        lax.fori_loop(0, nb // slots_at_once, one, 0)
        for h in range(2):
            s = (c, h)
            copies = []
            for e in (1, 3, 2):
                p = ring_add(c1[h], e)
                copy = remote(
                    bufs["send", s].at[p, pl.ds(0, nb)], bufs["got", s].at[e - 1, pl.ds(0, nb)],
                    sem_v, (c, h, e - 1), first(h, e),
                )
                copy.start()
                copies.append(copy)
            v_copies[s] = copies

    def reduce_send(s):
        c, h = s
        for copy in v_copies[s]:
            copy.wait_recv()
        for copy in p_copies.get(s, ()):
            copy.wait_send()
        mine_at = c1[h]

        def one(pos, _):
            t = table_of(h, 0)
            value = bufs["send", s][mine_at, table_s[t, 2 * h, pos]] + bufs["send", s][mine_at, table_s[t, 2 * h + 1, pos]]
            for e in range(1, RING):
                t = table_of(h, RING - e)
                value = value + bufs["got", s][e - 1, table_s[t, 2 * h, pos]]
                value = value + bufs["got", s][e - 1, table_s[t, 2 * h + 1, pos]]
            bufs["psum", s][pos] = value
            return 0

        lax.fori_loop(0, n_pos, one, 0, unroll=4)
        copies = []
        for e in (1, 3, 2):
            p = ring_add(c2[h], e)
            copy = remote(
                bufs["psum", s].at[pl.ds(pl.multiple_of(p * mine, mine), mine)], bufs["got2", s].at[e - 1],
                sem_p, (c, h, e - 1), second(h, e),
            )
            copy.start()
            copies.append(copy)
        p_copies[s] = copies

    def renew_send(s, moved):
        c, h = s
        for copy in p_copies[s]:
            copy.wait_recv()
        for copy in q_copies[s]:
            copy.wait_send()
        for k in range(mine):
            at = c2[h] * mine + k
            total = bufs["psum", s][at]
            for e in range(1, RING):
                total = total + bufs["got2", s][e - 1, k]
            count = count_s[h, at]
            new = total / jnp.maximum(count, 1.0)
            change = new - bufs["grid", s][at]
            moved = moved + count * (change * change)
            bufs["grid", s][at] = new
        q_copies[s] = send_grid(s)
        return moved

    for s in streams:
        w_copies[s] = gather_send(s, ())
    sums = []
    owner_copies = []
    for step in range(ITERS):
        for c in range(2):
            for h in range(2):
                for copy in w_copies[c, h]:
                    copy.wait_recv()
            primal = update(c, step)
            if step > 0:
                sums[2 * (step - 1)] = sums[2 * (step - 1)] + primal
            couple_send(c, step)
        if step == ITERS - 1:
            tail = pl.ds(bound, kkt.shape[0] - bound)
            state[tail] = base[tail] + jnp.dot(
                kkt[tail, 0:bound], drive[...], preferred_element_type=jnp.float32
            )
            state_out = pltpu.make_async_copy(state, state_ref, sem_local.at[12])
            state_out.start()
        for s in streams:
            reduce_send(s)
        moved = zero
        for s in streams:
            moved = renew_send(s, moved)
            if step == ITERS - 1:
                c, h = s
                for e in range(1, RING):
                    p = ring_add(c1[h], e)
                    at = pl.multiple_of(c2[h] * mine + p * owned, owned)
                    rows = pl.ds(pl.multiple_of(h * RING * ROWS + c1[h] * ROWS, ROWS), ROWS)
                    copy = remote(
                        bufs["grid", s].at[pl.ds(at, owned)], cons.at[:, rows, pl.ds(c * LANES, LANES)],
                        sem_o, (c, h, e - 1), first(h, e),
                    )
                    copy.start()
                    owner_copies.append(copy)
                rows = pl.ds(pl.multiple_of(h * RING * ROWS + c1[h] * ROWS, ROWS), ROWS)
                for o in range(owned):
                    cons[o, rows, c * LANES : (c + 1) * LANES] = bufs["grid", s][c2[h] * mine + c1[h] * owned + o]
        sums.append(zero)
        sums.append((penalty * penalty) * moved)
        for s in streams:
            w_copies[s] = gather_send(s, w_copies[s])
    for c in range(2):
        for h in range(2):
            for copy in w_copies[c, h]:
                copy.wait_recv()
        sums[2 * (ITERS - 1)] = sums[2 * (ITERS - 1)] + update(c, ITERS)
    dual_out = pltpu.make_async_copy(dual, duals_ref, sem_local.at[13])
    dual_out.start()

    tile = jnp.zeros((8, LANES), jnp.float32)
    for q, value in enumerate(sums):
        tile = jnp.where(row == q, jnp.sum(value, axis=0, keepdims=True), tile)
    totals_a[pl.ds(r, 1)] = tile[None]
    copies = []
    for e in range(1, n_region):
        copy = remote(totals_a.at[r], totals_a.at[r], sem_n, (e - 1,), lax.rem(r + e, n_region))
        copy.start()
        copies.append(copy)
    for copy in owner_copies:
        copy.wait()
    cons_out = pltpu.make_async_copy(cons, consensus_ref, sem_local.at[14])
    cons_out.start()
    for copy in copies:
        copy.wait()
    totals_b[pl.ds(sub, 1)] = jnp.sum(totals_a[...], axis=0, keepdims=True)
    copies = []
    for e in range(1, n_sub):
        copy = pltpu.make_async_remote_copy(
            src_ref=totals_b.at[sub], dst_ref=totals_b.at[sub],
            send_sem=sem_n.at[0, n_region - 2 + e], recv_sem=sem_n.at[1, n_region - 2 + e],
            device_id={"sub": lax.rem(sub + e, n_sub)}, device_id_type=MESH,
        )
        copy.start()
        copies.append(copy)
    for copy in copies:
        copy.wait()
    table = jnp.sum(jnp.sum(totals_b[...], axis=0), axis=1, keepdims=True)
    scale = 1.0 / (n_region * n_sub * 2 * LANES * BLOCK)
    norms_ref[...] = jnp.broadcast_to(jnp.sqrt(table * scale), (8, LANES))

    for s in streams:
        for copy in v_copies[s] + p_copies[s] + q_copies[s] + w_copies[s]:
            copy.wait_send()
    state_out.wait()
    dual_out.wait()
    cons_out.wait()


def shards(kkt_inverse, cost_terms, dual_start, consensus_start, block_target):
    order, scen = cost_terms.shape
    nb = block_target.shape[1]
    owned = consensus_start.shape[0] // BLOCK
    n_region = RING * RING
    n_sub = lax.axis_size("sub")
    n_pos = n_region * owned
    mine = RING * owned
    f32 = jnp.float32
    dma = pltpu.SemaphoreType.DMA
    per_stream = [
        pltpu.VMEM((RING, nb + 1, ROWS, LANES), f32),
        pltpu.VMEM((RING - 1, nb + 1, ROWS, LANES), f32),
        pltpu.VMEM((n_pos, ROWS, LANES), f32),
        pltpu.VMEM((RING - 1, mine, ROWS, LANES), f32),
        pltpu.VMEM((n_pos + 1, ROWS, LANES), f32),
        pltpu.VMEM((RING - 1, nb, ROWS, LANES), f32),
        pltpu.VMEM((RING - 1, nb, ROWS, LANES), f32),
        pltpu.VMEM((nb, ROWS, LANES), f32),
    ]
    state, duals, consensus, norms = pl.pallas_call(
        kernel,
        out_shape=(
            jax.ShapeDtypeStruct((order, scen), f32),
            jax.ShapeDtypeStruct((nb, BLOCK, scen), f32),
            jax.ShapeDtypeStruct((owned, BLOCK, scen), f32),
            jax.ShapeDtypeStruct((8, LANES), f32),
        ),
        in_specs=[pl.BlockSpec(memory_space=pl.ANY)] * 4 + [pl.BlockSpec(memory_space=pltpu.SMEM)],
        out_specs=(pl.BlockSpec(memory_space=pl.ANY),) * 3 + (pl.BlockSpec(memory_space=pltpu.VMEM),),
        scratch_shapes=[
            pltpu.VMEM((order, order), jnp.bfloat16),
            pltpu.VMEM((order, scen), jnp.bfloat16),
            pltpu.VMEM((order, scen), f32),
            pltpu.VMEM((order, scen), f32),
            pltpu.VMEM((nb, BLOCK, scen), f32),
            pltpu.VMEM((owned, BLOCK, scen), f32),
            pltpu.VMEM((nb * BLOCK, scen), jnp.bfloat16),
            pltpu.VMEM((n_region, 8, LANES), jnp.int32),
            pltpu.SMEM((2 * RING - 1, 8, LANES), jnp.int32),
            pltpu.VMEM((8, LANES), f32),
            pltpu.SMEM((8, LANES), f32),
            pltpu.VMEM((8, LANES), f32),
            pltpu.VMEM((n_region, 8, LANES), f32),
            pltpu.VMEM((n_sub, 8, LANES), f32),
        ]
        + per_stream * 4
        + [
            dma((15,)),
            dma((2, n_region - 1)),
            dma((2, 2, 2, RING - 1)),
            dma((2, 2, 2, RING - 1)),
            dma((2, 2, 2, RING - 1)),
            dma((2, 2, 2, RING - 1)),
            dma((2, 2, 2, RING - 1)),
            dma((2, 2, 2, RING - 1)),
            dma((2, n_region - 1 + n_sub - 1)),
        ],
        compiler_params=pltpu.CompilerParams(
            collective_id=0, has_side_effects=True, vmem_limit_bytes=60 * 2**20
        ),
        name="admm",
    )(
        kkt_inverse,
        cost_terms,
        dual_start.reshape(nb, BLOCK, scen),
        consensus_start.reshape(owned, BLOCK, scen),
        block_target,
    )
    return (
        state,
        duals.reshape(nb * BLOCK, scen),
        consensus.reshape(owned * BLOCK, scen),
        norms[: 2 * ITERS, 0].reshape(ITERS, 2),
    )


def solution(mesh):
    both = P(("region", "sub"), None)
    return jax.shard_map(
        shards, mesh=mesh, in_specs=(both,) * 5, out_specs=(both, both, both, P()), check_vma=False
    )
```

time: 475 us -> 109 us (0.23); the launches traced: 469 us -> 109 us
  waiting for transfers between devices: 230 us -> 0 us
  Pallas kernels: 0 us -> 102 us
  local copies, waits for them, and re-layouts: 76.9 us -> 6.45 us
  matrix products: 62.2 us -> 0 us
  starting transfers between devices: 50.2 us -> 0 us
  blocking collectives: 38.7 us -> 0 us
  other arithmetic: 7.64 us -> 0 us
    all_to_all x6 -> x0, waiting for transfers between devices: 230 us -> none  [the longest x3 133 us: fetch(): lax.all_to_all(reply, REGION, split_axis=0, concat_axis=0, tiled=True)]
    pallas_call x0 -> x1, Pallas kernels: none -> 102 us  [shards(): pl.pallas_call(kernel, out_shape=(jax.ShapeDtypeStruct((order, scen), f32...]
    dot_general x13 -> x0, matrix products: 62.2 us -> none  [the longest x3 19.2 us: fetch(): return jnp.dot(send_hot.T, back, precision=highest)]
    reshape x15 -> x0, local copies, waits for them, and re-layouts: 58.6 us -> none  [the longest x3 18.2 us: fetch(): lax.all_to_all(reply, REGION, split_axis=0, concat_axis=0, tiled=True)]
    all_to_all x6 -> x0, starting transfers between devices: 50.2 us -> none  [the longest x3 26.1 us: fetch(): lax.all_to_all(reply, REGION, split_axis=0, concat_axis=0, tiled=True)]
    psum x4 -> x0, blocking collectives: 38.7 us -> none  [one_axis_at_a_time(): shard = lax.psum(shard, axis)]
    dot_general x2 -> x0, local copies, waits for them, and re-layouts: 10.4 us -> none  [the longest x1 5.21 us: fetch(): jnp.dot(recv_hot.T, values, precision=highest).reshape(peers, CAP, -1)]
  transfers between devices with their start and end apart: 6 -> 0, of which waited for: 6 -> 0; matrix products, arithmetic and copies ran while one was open for 3% -> 0% of each run, Pallas kernels for 0% -> 0%
where the time goes in v1:
time: 109 us
  Pallas kernels  102 us (94%)
  local copies, waits for them, and re-layouts  6.45 us (6%)
    pallas_call x1, Pallas kernels, shards(): pl.pallas_call(kernel, out_shape=(jax.ShapeDtypeStruct((order, scen), f32...  102 us
    unnamed x7, local copies, waits for them, and re-layouts  5.02 us

profile of v1, /device:TPU:1, one launch (start us, length us, event | category | flops | bytes accessed | tf_op | source)
XLA Modules:
  0.0 108.9 jit_solution(11169140751221277960)
XLA Ops:
  0.6 101.8 %admm.1 = (f32[2048,256]{1,0:T(8,128)}, f32[12,128,256]{2,1,0:T(8,128)}, f32[2,128,256]{2,1,0:T(8,128)}, f32[8,128]{1,0:T(8,128)}) custom-call(bf16[2048,2048]{1,0:T(8,128)(2,1)} %kkt_ref.1, bf16[2048,256]{1,0:T(8,128)(2,1)} %cost_ref.1, f32[12,128,256]{2,1,0:T(8,128)} %bitcast.5, f32[2,128,256]{2,1,0:T(8,128)} %bitcast.6, s32[1,12]{1,0:T(1,128)} %target_ref.1), custom_call_target="tpu_custom_call" | custom-call | tf_op jit(solution)/shard_map/admm/pallas_call | solution.py:454
  102.5 0.8 slice_reduce_fusion
  103.2 0.6 reshape_squeeze.3
  103.9 0.0 copy-start
  103.9 3.2 %copy.12 = f32[2048,256]{1,0:T(8,128)} copy(f32[2048,256]{1,0:T(8,128)} %get-tuple-element.16) | data formatting | bytes 4194304
  107.1 0.0 copy-done
  107.1 0.0 copy-start.1
  107.1 1.1 %copy.13 = f32[1536,256]{1,0:T(8,128)} copy(f32[1536,256]{1,0:T(8,128)S(1)} %bitcast.4) | data formatting | bytes 3145728
  108.2 0.0 copy-done.1
  108.2 0.7 copy.14
Async XLA Ops:
  103.9 3.2 %copy-start = (f32[12,128,256]{2,1,0:T(8,128)S(1)}, f32[12,128,256]{2,1,0:T(8,128)}, u32[]{:S(2)}) copy-start(f32[12,128,256]{2,1,0:T(8,128)} %get-tuple-element.9) | copy-start | bytes 4718596
  107.1 1.1 %copy-start.1 = (f32[2,128,256]{2,1,0:T(8,128)S(1)}, f32[2,128,256]{2,1,0:T(8,128)}, u32[]{:S(2)}) copy-start(f32[2,128,256]{2,1,0:T(8,128)} %get-tuple-element.10) | copy-start | bytes 786436

commit v2 on v1

--- a/solution.py
+++ b/solution.py
@@ -22,8 +22,8 @@
 
 def kernel(
     kkt_ref, cost_ref, dual_ref, cons_ref, target_ref,
-    state_ref, duals_ref, consensus_ref, norms_ref,
-    kkt, cost, base, state, dual, cons, drive, tables, table_s, count_v, count_s, part, totals_a, totals_b,
+    state, dual, consensus, norms_ref,
+    kkt, cost, base, cons, drive, tables, table_s, partial_v, count_v, count_s, totals_a, totals_b,
     *rest,
 ):
     nb = target_ref.shape[1]
@@ -33,16 +33,14 @@
     n_pos = n_region * owned
     mine = RING * owned
     bound = nb * BLOCK
-    order = rest[0].shape[0]
     streams = [(c, h) for c in range(2) for h in range(2)]
     bufs = {}
-    names = ("send", "got", "psum", "got2", "grid", "back", "fetched", "own")
+    names = ("send", "got", "psum", "got2", "grid", "back", "fetched", "own", "held")
     rest = list(rest)
     for s in streams:
         for name in names:
             bufs[name, s] = rest.pop(0)
-    sem_local, sem_table, sem_init, sem_v, sem_p, sem_q, sem_w, sem_o, sem_n = rest
-    del order
+    sem_local, sem_table, sem_count, sem_init, sem_v, sem_p, sem_q, sem_w, sem_o, sem_n = rest
 
     r = lax.axis_index("region")
     sub = lax.axis_index("sub")
@@ -74,10 +72,9 @@
         copy.start()
 
     barrier = pltpu.get_barrier_semaphore()
-    for e in range(1, n_region):
-        pl.semaphore_signal(
-            barrier, inc=1, device_id={"region": lax.rem(r + e, n_region)}, device_id_type=MESH
-        )
+    near = [(h, e) for h in range(2) for e in range(1, RING)]
+    for h, e in near:
+        pl.semaphore_signal(barrier, inc=1, device_id={"region": first(h, e)}, device_id_type=MESH)
     for e in range(1, n_sub):
         pl.semaphore_signal(barrier, inc=1, device_id={"sub": lax.rem(sub + e, n_sub)}, device_id_type=MESH)
 
@@ -103,7 +100,7 @@
     tile = jnp.where(row == 1, two_a, tile)
     tile = jnp.where(row == 2, one_b, tile)
     tile = jnp.where(row == 3, two_b, tile)
-    tables[pl.ds(r, 1)] = tile[None]
+    tables[0] = tile
 
     zero = jnp.zeros((ROWS, LANES), jnp.float32)
     for s in streams:
@@ -114,7 +111,7 @@
         bufs["grid", s][n_pos] = zero
 
     local[0].wait()
-    pl.semaphore_wait(barrier, n_region - 1 + n_sub - 1)
+    pl.semaphore_wait(barrier, len(near) + n_sub - 1)
 
     init = {}
     for s in streams:
@@ -126,8 +123,9 @@
             init[s, e] = remote(src, bufs["grid", s].at[pl.ds(at, owned)], sem_init, (c, h, e - 1), first(h, e))
             init[s, e].start()
     table_copies = []
-    for e in range(1, n_region):
-        copy = remote(tables.at[r], tables.at[r], sem_table, (e - 1,), lax.rem(r + e, n_region))
+    for h, e in near:
+        i = (RING - 1) * h + e
+        copy = remote(tables.at[0], tables.at[i], sem_table, (i,), first(h, e))
         copy.start()
         table_copies.append(copy)
     for s in streams:
@@ -156,25 +154,30 @@
 
     for copy in table_copies:
         copy.wait()
-    peers = [r] + [first(0, e) for e in range(1, RING)] + [first(1, e) for e in range(1, RING)]
-    moves = [
-        pltpu.make_async_copy(tables.at[peer], table_s.at[i], sem_local.at[4 + i]) for i, peer in enumerate(peers)
-    ]
-    for move in moves:
-        move.start()
-    every = tables[...]
-    used = jnp.sum((every < nb).astype(jnp.int32), axis=0).astype(jnp.float32)
-    count_a = used[0:1] + used[1:2]
-    count_b = used[2:3] + used[3:4]
-    count_v[...] = jnp.where(row == 0, count_a, count_b)
-    counting = pltpu.make_async_copy(count_v, count_s, sem_local.at[11])
-    counting.start()
-    for move in moves:
-        move.wait()
-    counting.wait()
+    to_scalar = pltpu.make_async_copy(tables, table_s, sem_local.at[4])
+    to_scalar.start()
+
+    def uses(i, h):
+        hits = (tables[i] < nb).astype(jnp.float32)
+        return hits[2 * h : 2 * h + 1] + hits[2 * h + 1 : 2 * h + 2]
+
+    over = []
+    for h in range(2):
+        total = uses(0, h)
+        for e in range(1, RING):
+            total = total + uses((RING - 1) * h + e, h)
+        over.append(total)
+    partial_v[0] = jnp.where(row == 0, over[0], over[1])
+    count_copies = []
+    for h, e in near:
+        i = (RING - 1) * h + e
+        copy = remote(partial_v.at[0], partial_v.at[i], sem_count, (i,), first(h, e))
+        copy.start()
+        count_copies.append(copy)
+    to_scalar.wait()
 
     def table_of(h, e):
-        return 0 if e == 0 else (e if h == 0 else RING - 1 + e)
+        return 0 if e == 0 else (RING - 1) * h + e
 
     def live(s):
         return jnp.where(target_ref[0, s] >= 0, 1.0, 0.0).astype(jnp.float32)
@@ -192,42 +195,59 @@
     lax.fori_loop(0, kkt.shape[0] // half, base_rows, 0)
     local[2].wait()
 
-    def gather_send(s, before):
+    for copy in count_copies:
+        copy.wait()
+    count_a = partial_v[0, 0:1] + partial_v[RING, 0:1]
+    count_b = partial_v[0, 1:2] + partial_v[1, 1:2]
+    for e in range(2, RING):
+        count_a = count_a + partial_v[RING - 1 + e, 0:1]
+        count_b = count_b + partial_v[e, 1:2]
+    count_v[...] = jnp.where(row == 0, count_a, count_b)
+    counting = pltpu.make_async_copy(count_v, count_s, sem_local.at[5])
+    counting.start()
+    counting.wait()
+
+    def gather(s, before, step, primal):
         c, h = s
         for copy in q_copies[s]:
             copy.wait_recv()
         for copy in before:
             copy.wait_send()
-        copies = []
         grid = bufs["grid", s]
         for e in (1, 3, 2, 0):
-            t = table_of(h, e)
-
-            def one(slot, _):
-                value = grid[table_s[t, 4 + h, slot]]
+            back = 0 if e == 0 else RING - e
+            t = table_of(h, back)
+
+            def one(slot, primal):
+                place = table_s[t, 4 + h, slot]
+                value = grid[place]
                 if e:
                     bufs["back", s][e - 1, slot] = value
                 else:
                     bufs["own", s][slot] = value
-                return 0
-
-            lax.fori_loop(0, nb, one, 0, unroll=4)
-            if e:
-                copy = remote(
-                    bufs["back", s].at[e - 1], bufs["fetched", s].at[e - 1], sem_w, (c, h, e - 1), first(h, e)
-                )
-                copy.start()
-                copies.append(copy)
+                if step:
+                    sent = bufs["got", s][back - 1, slot] if e else bufs["send", s][c1[h], slot]
+                    if step == 1:
+                        bufs["held", s][e, slot] = sent - value
+                    else:
+                        alive = jnp.where(place < n_pos, 1.0, 0.0).astype(jnp.float32)
+                        gap = sent - bufs["held", s][e, slot] - value
+                        primal = primal + alive * (gap * gap)
+                return primal
+
+            primal = lax.fori_loop(0, nb, one, primal, unroll=4)
+        return primal
+
+    def back_send(s):
+        c, h = s
+        copies = []
+        for e in (1, 3, 2):
+            copy = remote(
+                bufs["back", s].at[e - 1], bufs["fetched", s].at[e - 1], sem_w, (c, h, e - 1), first(h, e)
+            )
+            copy.start()
+            copies.append(copy)
         return copies
-
-    def fetched_rows(s, slot, p):
-        c, h = s
-        return bufs["fetched", s][lax.rem(c1[h] - p + RING, RING), slot]
-
-    def own_into_place(s):
-        pass
-
-    part_primal = {}
 
     def update(c, step):
         cols = pl.ds(c * LANES, LANES)
@@ -244,7 +264,8 @@
                     at = pl.ds(pl.multiple_of(slot * BLOCK + h * RING * ROWS + p * ROWS, ROWS), ROWS)
                     if step > 0:
                         gap = state[at, cols] - value
-                        total = total + alive * gap * gap
+                        if step < ITERS:
+                            total = total + alive * (gap * gap)
                         old = old + alive * gap
                         dual[slot, in_block, cols] = old
                     if step < ITERS:
@@ -303,7 +324,7 @@
             t = table_of(h, 0)
             value = bufs["send", s][mine_at, table_s[t, 2 * h, pos]] + bufs["send", s][mine_at, table_s[t, 2 * h + 1, pos]]
             for e in range(1, RING):
-                t = table_of(h, RING - e)
+                t = table_of(h, e)
                 value = value + bufs["got", s][e - 1, table_s[t, 2 * h, pos]]
                 value = value + bufs["got", s][e - 1, table_s[t, 2 * h + 1, pos]]
             bufs["psum", s][pos] = value
@@ -341,31 +362,31 @@
         return moved
 
     for s in streams:
-        w_copies[s] = gather_send(s, ())
-    sums = []
+        gather(s, (), 0, zero)
+        w_copies[s] = back_send(s)
+    primal = [zero] * ITERS
+    moved = [zero] * ITERS
     owner_copies = []
     for step in range(ITERS):
+        last = step == ITERS - 1
         for c in range(2):
             for h in range(2):
                 for copy in w_copies[c, h]:
                     copy.wait_recv()
-            primal = update(c, step)
+            got = update(c, step)
             if step > 0:
-                sums[2 * (step - 1)] = sums[2 * (step - 1)] + primal
+                primal[step - 1] = primal[step - 1] + got
             couple_send(c, step)
-        if step == ITERS - 1:
+        if last:
             tail = pl.ds(bound, kkt.shape[0] - bound)
             state[tail] = base[tail] + jnp.dot(
                 kkt[tail, 0:bound], drive[...], preferred_element_type=jnp.float32
             )
-            state_out = pltpu.make_async_copy(state, state_ref, sem_local.at[12])
-            state_out.start()
         for s in streams:
             reduce_send(s)
-        moved = zero
         for s in streams:
-            moved = renew_send(s, moved)
-            if step == ITERS - 1:
+            moved[step] = renew_send(s, moved[step])
+            if last:
                 c, h = s
                 for e in range(1, RING):
                     p = ring_add(c1[h], e)
@@ -380,35 +401,30 @@
                 rows = pl.ds(pl.multiple_of(h * RING * ROWS + c1[h] * ROWS, ROWS), ROWS)
                 for o in range(owned):
                     cons[o, rows, c * LANES : (c + 1) * LANES] = bufs["grid", s][c2[h] * mine + c1[h] * owned + o]
-        sums.append(zero)
-        sums.append((penalty * penalty) * moved)
-        for s in streams:
-            w_copies[s] = gather_send(s, w_copies[s])
-    for c in range(2):
-        for h in range(2):
-            for copy in w_copies[c, h]:
-                copy.wait_recv()
-        sums[2 * (ITERS - 1)] = sums[2 * (ITERS - 1)] + update(c, ITERS)
-    dual_out = pltpu.make_async_copy(dual, duals_ref, sem_local.at[13])
-    dual_out.start()
+        for c in range(2):
+            for h in range(2):
+                s = (c, h)
+                primal[step] = gather(s, w_copies[s], step + 1, primal[step])
+                if not (last and c == 1):
+                    w_copies[s] = back_send(s)
 
     tile = jnp.zeros((8, LANES), jnp.float32)
-    for q, value in enumerate(sums):
-        tile = jnp.where(row == q, jnp.sum(value, axis=0, keepdims=True), tile)
+    for step in range(ITERS):
+        tile = jnp.where(row == 2 * step, jnp.sum(primal[step], axis=0, keepdims=True), tile)
+        change = (penalty * penalty) * jnp.sum(moved[step], axis=0, keepdims=True)
+        tile = jnp.where(row == 2 * step + 1, change, tile)
     totals_a[pl.ds(r, 1)] = tile[None]
-    copies = []
+    norm_copies = []
     for e in range(1, n_region):
         copy = remote(totals_a.at[r], totals_a.at[r], sem_n, (e - 1,), lax.rem(r + e, n_region))
         copy.start()
-        copies.append(copy)
-    for copy in owner_copies:
-        copy.wait()
-    cons_out = pltpu.make_async_copy(cons, consensus_ref, sem_local.at[14])
-    cons_out.start()
-    for copy in copies:
+        norm_copies.append(copy)
+    for h in range(2):
+        w_copies[1, h] = back_send((1, h))
+    for copy in norm_copies:
         copy.wait()
     totals_b[pl.ds(sub, 1)] = jnp.sum(totals_a[...], axis=0, keepdims=True)
-    copies = []
+    norm_copies = []
     for e in range(1, n_sub):
         copy = pltpu.make_async_remote_copy(
             src_ref=totals_b.at[sub], dst_ref=totals_b.at[sub],
@@ -416,19 +432,41 @@
             device_id={"sub": lax.rem(sub + e, n_sub)}, device_id_type=MESH,
         )
         copy.start()
-        copies.append(copy)
-    for copy in copies:
+        norm_copies.append(copy)
+
+    for copy in owner_copies:
+        copy.wait()
+    consensus[...] = cons[...]
+    for c in range(2):
+        for h in range(2):
+            for copy in w_copies[c, h]:
+                copy.wait_recv()
+        update(c, ITERS)
+    for copy in norm_copies:
         copy.wait()
     table = jnp.sum(jnp.sum(totals_b[...], axis=0), axis=1, keepdims=True)
     scale = 1.0 / (n_region * n_sub * 2 * LANES * BLOCK)
-    norms_ref[...] = jnp.broadcast_to(jnp.sqrt(table * scale), (8, LANES))
+    table = jnp.sqrt(table * scale)
+    small = (ITERS, 2)
+    which = lax.broadcasted_iota(jnp.int32, small, 0) * 2 + lax.broadcasted_iota(jnp.int32, small, 1)
+    norms = jnp.zeros(small, jnp.float32)
+    for q in range(2 * ITERS):
+        norms = jnp.where(which == q, jnp.broadcast_to(table[q : q + 1], small), norms)
+    norms_ref[...] = norms
 
     for s in streams:
         for copy in v_copies[s] + p_copies[s] + q_copies[s] + w_copies[s]:
             copy.wait_send()
-    state_out.wait()
-    dual_out.wait()
-    cons_out.wait()
+
+
+def put_out(*refs):
+    *arrays, sems = refs
+    count = len(arrays) // 2
+    copies = [pltpu.make_async_copy(arrays[i], arrays[count + i], sems.at[i]) for i in range(count)]
+    for copy in copies:
+        copy.start()
+    for copy in copies:
+        copy.wait()
 
 
 def shards(kkt_inverse, cost_terms, dual_start, consensus_start, block_target):
@@ -450,37 +488,37 @@
         pltpu.VMEM((RING - 1, nb, ROWS, LANES), f32),
         pltpu.VMEM((RING - 1, nb, ROWS, LANES), f32),
         pltpu.VMEM((nb, ROWS, LANES), f32),
+        pltpu.VMEM((RING, nb, ROWS, LANES), f32),
     ]
     state, duals, consensus, norms = pl.pallas_call(
         kernel,
         out_shape=(
-            jax.ShapeDtypeStruct((order, scen), f32),
-            jax.ShapeDtypeStruct((nb, BLOCK, scen), f32),
-            jax.ShapeDtypeStruct((owned, BLOCK, scen), f32),
-            jax.ShapeDtypeStruct((8, LANES), f32),
+            pltpu.VMEM((order, scen), f32),
+            pltpu.VMEM((nb, BLOCK, scen), f32),
+            pltpu.VMEM((owned, BLOCK, scen), f32),
+            pltpu.VMEM((ITERS, 2), f32),
         ),
-        in_specs=[pl.BlockSpec(memory_space=pl.ANY)] * 4 + [pl.BlockSpec(memory_space=pltpu.SMEM)],
-        out_specs=(pl.BlockSpec(memory_space=pl.ANY),) * 3 + (pl.BlockSpec(memory_space=pltpu.VMEM),),
+        in_specs=[pl.BlockSpec(memory_space=pltpu.HBM)] * 4 + [pl.BlockSpec(memory_space=pltpu.SMEM)],
+        out_specs=(pl.BlockSpec(memory_space=pltpu.VMEM),) * 4,
         scratch_shapes=[
             pltpu.VMEM((order, order), jnp.bfloat16),
             pltpu.VMEM((order, scen), jnp.bfloat16),
             pltpu.VMEM((order, scen), f32),
-            pltpu.VMEM((order, scen), f32),
-            pltpu.VMEM((nb, BLOCK, scen), f32),
             pltpu.VMEM((owned, BLOCK, scen), f32),
             pltpu.VMEM((nb * BLOCK, scen), jnp.bfloat16),
-            pltpu.VMEM((n_region, 8, LANES), jnp.int32),
+            pltpu.VMEM((2 * RING - 1, 8, LANES), jnp.int32),
             pltpu.SMEM((2 * RING - 1, 8, LANES), jnp.int32),
+            pltpu.VMEM((2 * RING - 1, 8, LANES), f32),
             pltpu.VMEM((8, LANES), f32),
             pltpu.SMEM((8, LANES), f32),
-            pltpu.VMEM((8, LANES), f32),
             pltpu.VMEM((n_region, 8, LANES), f32),
             pltpu.VMEM((n_sub, 8, LANES), f32),
         ]
         + per_stream * 4
         + [
-            dma((15,)),
-            dma((2, n_region - 1)),
+            dma((6,)),
+            dma((2, 2 * RING - 1)),
+            dma((2, 2 * RING - 1)),
             dma((2, 2, 2, RING - 1)),
             dma((2, 2, 2, RING - 1)),
             dma((2, 2, 2, RING - 1)),
@@ -490,22 +528,36 @@
             dma((2, n_region - 1 + n_sub - 1)),
         ],
         compiler_params=pltpu.CompilerParams(
-            collective_id=0, has_side_effects=True, vmem_limit_bytes=60 * 2**20
+            collective_id=0, has_side_effects=True, vmem_limit_bytes=40 * 2**20
         ),
         name="admm",
     )(
-        kkt_inverse,
-        cost_terms,
-        dual_start.reshape(nb, BLOCK, scen),
-        consensus_start.reshape(owned, BLOCK, scen),
-        block_target,
+        *(
+            pltpu.with_memory_space_constraint(a, pltpu.HBM)
+            for a in (
+                kkt_inverse,
+                cost_terms,
+                dual_start.reshape(nb, BLOCK, scen),
+                consensus_start.reshape(owned, BLOCK, scen),
+                block_target,
+            )
+        )
     )
-    return (
+    results = (
         state,
         duals.reshape(nb * BLOCK, scen),
         consensus.reshape(owned * BLOCK, scen),
-        norms[: 2 * ITERS, 0].reshape(ITERS, 2),
+        norms,
     )
+    return pl.pallas_call(
+        put_out,
+        out_shape=tuple(jax.ShapeDtypeStruct(a.shape, a.dtype) for a in results),
+        in_specs=[pl.BlockSpec(memory_space=pltpu.VMEM)] * len(results),
+        out_specs=(pl.BlockSpec(memory_space=pl.ANY),) * len(results),
+        scratch_shapes=[dma((len(results),))],
+        name="put_out",
+        compiler_params=pltpu.CompilerParams(vmem_limit_bytes=8 * 2**20),
+    )(*(pltpu.with_memory_space_constraint(a, pltpu.VMEM) for a in results))
 
 
 def solution(mesh):

time: 109 us -> 98.8 us (0.906)
  local copies, waits for them, and re-layouts: 6.45 us -> 0 us
  Pallas kernels: 102 us -> 98.1 us
    unnamed x7 -> x0, local copies, waits for them, and re-layouts: 5.02 us -> none
    pallas_call x1 -> x2, Pallas kernels: 102 us -> 98.1 us  [the longest x1 96.1 us: shards(): pl.pallas_call(kernel, out_shape=(pltpu.VMEM((order, scen), f32), pltpu.V...]
where the time goes in v2:
time: 98.8 us; the launch traced here: 98.7 us
  Pallas kernels  98.1 us (99%)
    pallas_call x1, Pallas kernels, shards(): pl.pallas_call(kernel, out_shape=(pltpu.VMEM((order, scen), f32), pltpu.V...  96.1 us

profile of v2, /device:TPU:1, one launch (start us, length us, event | category | flops | bytes accessed | tf_op | source)
XLA Modules:
  0.0 98.7 jit_solution(14165797010543202646)
XLA Ops:
  0.6 96.1 %admm.1 = (f32[2048,256]{1,0:T(8,128)S(1)}, f32[12,128,256]{2,1,0:T(8,128)S(1)}, f32[2,128,256]{2,1,0:T(8,128)S(1)}, f32[2,2]{1,0:T(2,128)S(1)}) custom-call(bf16[2048,2048]{1,0:T(8,128)(2,1)} %kkt_ref.1, bf16[2048,256]{1,0:T(8,128)(2,1)} %cost_ref.1, f32[12,128,256]{2,1,0:T(8,128)} %bitcast.6, f32[2,128,256]{2,1,0:T(8,128)} %bitcast.7, s32[1,12]{1,0:T(1,128)} %target_ref.1), custom_call_target="tpu_custom_call" | custom-call | tf_op jit(solution)/shard_map/admm/pallas_call | solution.py:493
  96.8 1.9 %put_out.1 = (f32[2048,256]{1,0:T(8,128)}, f32[1536,256]{1,0:T(8,128)}, f32[256,256]{1,0:T(8,128)}, f32[2,2]{1,0:T(2,128)}) custom-call(f32[2048,256]{1,0:T(8,128)S(1)} %get-tuple-element.8.refs_0_, f32[1536,256]{1,0:T(8,128)S(1)} %bitcast.4, f32[256,256]{1,0:T(8,128)S(1)} %bitcast.5, f32[2,2]{1,0:T(2,128)S(1)} %get-tuple-element.11.refs_3_), custom_call_target="tpu_custom_call" | custom-call | tf_op jit(solution)/shard_map/put_out/pallas_call | solution.py:552

commit v3 on v2

--- a/solution.py
+++ b/solution.py
@@ -11,7 +11,8 @@
 BLOCK = 128
 ITERS = 2
 RING = 4
-ROWS = 16
+QUARTERS = 4
+ROWS = 8
 LANES = 128
 penalty = 1.5
 
@@ -21,21 +22,21 @@
 
 
 def kernel(
-    kkt_ref, cost_ref, dual_ref, cons_ref, target_ref,
+    kkt_ref, cost_ref, dual_ref, cons_ref, target_hbm,
     state, dual, consensus, norms_ref,
-    kkt, cost, base, cons, drive, tables, table_s, partial_v, count_v, count_s, totals_a, totals_b,
+    target_ref, kkt, cost, base, cons, drive, tables, table_s, partial_v, count_v, count_s, totals_a, totals_b,
     *rest,
 ):
-    nb = target_ref.shape[1]
+    nb = target_hbm.shape[1]
     owned = cons_ref.shape[0]
     n_region = RING * RING
     n_sub = lax.axis_size("sub")
     n_pos = n_region * owned
     mine = RING * owned
     bound = nb * BLOCK
-    streams = [(c, h) for c in range(2) for h in range(2)]
+    streams = [(c, q) for c in range(2) for q in range(QUARTERS)]
     bufs = {}
-    names = ("send", "got", "psum", "got2", "grid", "back", "fetched", "own", "held")
+    names = ("send", "got", "psum", "got2", "grid", "back", "fetched", "held")
     rest = list(rest)
     for s in streams:
         for name in names:
@@ -63,12 +64,13 @@
         )
 
     local = [
+        pltpu.make_async_copy(target_hbm, target_ref, sem_local.at[6]),
         pltpu.make_async_copy(cons_ref, cons, sem_local.at[0]),
         pltpu.make_async_copy(cost_ref, cost, sem_local.at[1]),
         pltpu.make_async_copy(dual_ref, dual, sem_local.at[2]),
         pltpu.make_async_copy(kkt_ref, kkt, sem_local.at[3]),
     ]
-    for copy in local:
+    for copy in local[:2]:
         copy.start()
 
     barrier = pltpu.get_barrier_semaphore()
@@ -78,6 +80,7 @@
     for e in range(1, n_sub):
         pl.semaphore_signal(barrier, inc=1, device_id={"sub": lax.rem(sub + e, n_sub)}, device_id_type=MESH)
 
+    local[0].wait()
     lane = lax.broadcasted_iota(jnp.int32, (8, LANES), 1)
     row = lax.broadcasted_iota(jnp.int32, (8, LANES), 0)
     none = jnp.full((8, LANES), nb, jnp.int32)
@@ -110,17 +113,21 @@
             bufs["got", s][p, nb] = zero
         bufs["grid", s][n_pos] = zero
 
-    local[0].wait()
+    local[1].wait()
     pl.semaphore_wait(barrier, len(near) + n_sub - 1)
 
+    def shard_rows(q, p):
+        return pl.ds(pl.multiple_of((q * RING + p) * ROWS, ROWS), ROWS)
+
     init = {}
     for s in streams:
-        c, h = s
+        c, q = s
+        h = q % 2
         for e in range(1, RING):
             p = ring_add(c1[h], e)
             at = pl.multiple_of(c2[h] * mine + c1[h] * owned, owned)
-            src = cons.at[:, pl.ds(pl.multiple_of(h * RING * ROWS + p * ROWS, ROWS), ROWS), pl.ds(c * LANES, LANES)]
-            init[s, e] = remote(src, bufs["grid", s].at[pl.ds(at, owned)], sem_init, (c, h, e - 1), first(h, e))
+            src = cons.at[:, shard_rows(q, p), pl.ds(c * LANES, LANES)]
+            init[s, e] = remote(src, bufs["grid", s].at[pl.ds(at, owned)], sem_init, (c, q, e - 1), first(h, e))
             init[s, e].start()
     table_copies = []
     for h, e in near:
@@ -128,19 +135,23 @@
         copy = remote(tables.at[0], tables.at[i], sem_table, (i,), first(h, e))
         copy.start()
         table_copies.append(copy)
-    for s in streams:
-        c, h = s
+    for copy in local[2:]:
+        copy.start()
+    for s in streams:
+        c, q = s
+        h = q % 2
         for o in range(owned):
-            rows = pl.ds(pl.multiple_of(h * RING * ROWS + c1[h] * ROWS, ROWS), ROWS)
-            bufs["grid", s][c2[h] * mine + c1[h] * owned + o] = cons[o, rows, c * LANES : (c + 1) * LANES]
+            at = c2[h] * mine + c1[h] * owned + o
+            bufs["grid", s][at] = cons[o, shard_rows(q, c1[h]), c * LANES : (c + 1) * LANES]
 
     def send_grid(s):
-        c, h = s
+        c, q = s
+        h = q % 2
         copies = []
         at = pl.ds(pl.multiple_of(c2[h] * mine, mine), mine)
         for e in range(1, RING):
             copy = remote(
-                bufs["grid", s].at[at], bufs["grid", s].at[at], sem_q, (c, h, e - 1), second(h, e)
+                bufs["grid", s].at[at], bufs["grid", s].at[at], sem_q, (c, q, e - 1), second(h, e)
             )
             copy.start()
             copies.append(copy)
@@ -182,33 +193,9 @@
     def live(s):
         return jnp.where(target_ref[0, s] >= 0, 1.0, 0.0).astype(jnp.float32)
 
-    local[1].wait()
-    local[3].wait()
-
-    half = 256
-
-    def base_rows(i, _):
-        at = pl.ds(pl.multiple_of(i * half, half), half)
-        base[at] = jnp.dot(kkt[at], cost[...], preferred_element_type=jnp.float32)
-        return 0
-
-    lax.fori_loop(0, kkt.shape[0] // half, base_rows, 0)
-    local[2].wait()
-
-    for copy in count_copies:
-        copy.wait()
-    count_a = partial_v[0, 0:1] + partial_v[RING, 0:1]
-    count_b = partial_v[0, 1:2] + partial_v[1, 1:2]
-    for e in range(2, RING):
-        count_a = count_a + partial_v[RING - 1 + e, 0:1]
-        count_b = count_b + partial_v[e, 1:2]
-    count_v[...] = jnp.where(row == 0, count_a, count_b)
-    counting = pltpu.make_async_copy(count_v, count_s, sem_local.at[5])
-    counting.start()
-    counting.wait()
-
     def gather(s, before, step, primal):
-        c, h = s
+        c, q = s
+        h = q % 2
         for copy in q_copies[s]:
             copy.wait_recv()
         for copy in before:
@@ -224,7 +211,7 @@
                 if e:
                     bufs["back", s][e - 1, slot] = value
                 else:
-                    bufs["own", s][slot] = value
+                    bufs["fetched", s][0, slot] = value
                 if step:
                     sent = bufs["got", s][back - 1, slot] if e else bufs["send", s][c1[h], slot]
                     if step == 1:
@@ -239,11 +226,12 @@
         return primal
 
     def back_send(s):
-        c, h = s
+        c, q = s
+        h = q % 2
         copies = []
         for e in (1, 3, 2):
             copy = remote(
-                bufs["back", s].at[e - 1], bufs["fetched", s].at[e - 1], sem_w, (c, h, e - 1), first(h, e)
+                bufs["back", s].at[e - 1], bufs["fetched", s].at[e], sem_w, (c, q, e - 1), first(h, e)
             )
             copy.start()
             copies.append(copy)
@@ -254,14 +242,15 @@
 
         def one(slot, total):
             alive = live(slot)
-            for h in range(2):
-                s = (c, h)
-                for e in range(RING):
-                    p = lax.rem(c1[h] - e + RING, RING)
-                    value = bufs["own", s][slot] if e == 0 else bufs["fetched", s][e - 1, slot]
-                    in_block = pl.ds(pl.multiple_of(h * RING * ROWS + p * ROWS, ROWS), ROWS)
+            for q in range(QUARTERS):
+                for p in range(0, RING, 2):
+                    value = jnp.concatenate(
+                        [bufs["fetched", (c, q)][lax.rem(c1[q % 2] - p - i + RING, RING), slot] for i in range(2)]
+                    )
+                    lo = (q * RING + p) * ROWS
+                    in_block = pl.ds(lo, 2 * ROWS)
                     old = dual[slot, in_block, cols]
-                    at = pl.ds(pl.multiple_of(slot * BLOCK + h * RING * ROWS + p * ROWS, ROWS), ROWS)
+                    at = pl.ds(pl.multiple_of(slot * BLOCK + lo, 2 * ROWS), 2 * ROWS)
                     if step > 0:
                         gap = state[at, cols] - value
                         if step < ITERS:
@@ -272,15 +261,24 @@
                         drive[at, cols] = (penalty * alive * (value - old)).astype(jnp.bfloat16)
             return total
 
-        return lax.fori_loop(0, nb, one, jnp.zeros((ROWS, LANES), jnp.float32))
+        total = lax.fori_loop(0, nb, one, jnp.zeros((2 * ROWS, LANES), jnp.float32))
+        return total[:ROWS] + total[ROWS:]
 
     slots_at_once = 4
     chunk = slots_at_once * BLOCK
 
+    def sent(s, e, slots):
+        c, q = s
+        h = q % 2
+        return remote(
+            bufs["send", s].at[ring_add(c1[h], e), slots], bufs["got", s].at[e - 1, slots],
+            sem_v, (c, q, e - 1), first(h, e),
+        )
+
     def couple_send(c, step):
         cols = pl.ds(c * LANES, LANES)
-        for h in range(2):
-            for copy in v_copies.get((c, h), ()):
+        for q in range(QUARTERS):
+            for copy in v_copies.get((c, q), ()):
                 copy.wait_send()
 
         def one(i, _):
@@ -292,28 +290,22 @@
             for j in range(slots_at_once):
                 slot = i * slots_at_once + j
                 v = rows[j * BLOCK : (j + 1) * BLOCK] + dual[slot, :, cols]
-                for h in range(2):
+                for q in range(QUARTERS):
                     for p in range(RING):
-                        lo = h * RING * ROWS + p * ROWS
-                        bufs["send", (c, h)][p, slot] = v[lo : lo + ROWS]
+                        lo = (q * RING + p) * ROWS
+                        bufs["send", (c, q)][p, slot] = v[lo : lo + ROWS]
+            for q in range(QUARTERS):
+                for e in (1, 3, 2):
+                    sent((c, q), e, pl.ds(i * slots_at_once, slots_at_once)).start()
             return 0
 
         lax.fori_loop(0, nb // slots_at_once, one, 0)
-        for h in range(2):
-            s = (c, h)
-            copies = []
-            for e in (1, 3, 2):
-                p = ring_add(c1[h], e)
-                copy = remote(
-                    bufs["send", s].at[p, pl.ds(0, nb)], bufs["got", s].at[e - 1, pl.ds(0, nb)],
-                    sem_v, (c, h, e - 1), first(h, e),
-                )
-                copy.start()
-                copies.append(copy)
-            v_copies[s] = copies
+        for q in range(QUARTERS):
+            v_copies[c, q] = [sent((c, q), e, pl.ds(0, nb)) for e in (1, 3, 2)]
 
     def reduce_send(s):
-        c, h = s
+        c, q = s
+        h = q % 2
         for copy in v_copies[s]:
             copy.wait_recv()
         for copy in p_copies.get(s, ()):
@@ -330,20 +322,21 @@
             bufs["psum", s][pos] = value
             return 0
 
-        lax.fori_loop(0, n_pos, one, 0, unroll=4)
+        lax.fori_loop(0, n_pos, one, 0, unroll=8)
         copies = []
         for e in (1, 3, 2):
             p = ring_add(c2[h], e)
             copy = remote(
                 bufs["psum", s].at[pl.ds(pl.multiple_of(p * mine, mine), mine)], bufs["got2", s].at[e - 1],
-                sem_p, (c, h, e - 1), second(h, e),
+                sem_p, (c, q, e - 1), second(h, e),
             )
             copy.start()
             copies.append(copy)
         p_copies[s] = copies
 
     def renew_send(s, moved):
-        c, h = s
+        c, q = s
+        h = q % 2
         for copy in p_copies[s]:
             copy.wait_recv()
         for copy in q_copies[s]:
@@ -364,14 +357,39 @@
     for s in streams:
         gather(s, (), 0, zero)
         w_copies[s] = back_send(s)
+    local[2].wait()
+    local[4].wait()
+
+    half = 256
+
+    def base_rows(i, _):
+        at = pl.ds(pl.multiple_of(i * half, half), half)
+        base[at] = jnp.dot(kkt[at], cost[...], preferred_element_type=jnp.float32)
+        return 0
+
+    lax.fori_loop(0, kkt.shape[0] // half, base_rows, 0)
+    local[3].wait()
+
+    for copy in count_copies:
+        copy.wait()
+    count_a = partial_v[0, 0:1] + partial_v[RING, 0:1]
+    count_b = partial_v[0, 1:2] + partial_v[1, 1:2]
+    for e in range(2, RING):
+        count_a = count_a + partial_v[RING - 1 + e, 0:1]
+        count_b = count_b + partial_v[e, 1:2]
+    count_v[...] = jnp.where(row == 0, count_a, count_b)
+    counting = pltpu.make_async_copy(count_v, count_s, sem_local.at[5])
+    counting.start()
+    counting.wait()
+
     primal = [zero] * ITERS
     moved = [zero] * ITERS
     owner_copies = []
     for step in range(ITERS):
         last = step == ITERS - 1
         for c in range(2):
-            for h in range(2):
-                for copy in w_copies[c, h]:
+            for q in range(QUARTERS):
+                for copy in w_copies[c, q]:
                     copy.wait_recv()
             got = update(c, step)
             if step > 0:
@@ -387,23 +405,24 @@
         for s in streams:
             moved[step] = renew_send(s, moved[step])
             if last:
-                c, h = s
+                c, q = s
+                h = q % 2
                 for e in range(1, RING):
                     p = ring_add(c1[h], e)
                     at = pl.multiple_of(c2[h] * mine + p * owned, owned)
-                    rows = pl.ds(pl.multiple_of(h * RING * ROWS + c1[h] * ROWS, ROWS), ROWS)
                     copy = remote(
-                        bufs["grid", s].at[pl.ds(at, owned)], cons.at[:, rows, pl.ds(c * LANES, LANES)],
-                        sem_o, (c, h, e - 1), first(h, e),
+                        bufs["grid", s].at[pl.ds(at, owned)],
+                        cons.at[:, shard_rows(q, c1[h]), pl.ds(c * LANES, LANES)],
+                        sem_o, (c, q, e - 1), first(h, e),
                     )
                     copy.start()
                     owner_copies.append(copy)
-                rows = pl.ds(pl.multiple_of(h * RING * ROWS + c1[h] * ROWS, ROWS), ROWS)
                 for o in range(owned):
-                    cons[o, rows, c * LANES : (c + 1) * LANES] = bufs["grid", s][c2[h] * mine + c1[h] * owned + o]
+                    at = c2[h] * mine + c1[h] * owned + o
+                    cons[o, shard_rows(q, c1[h]), c * LANES : (c + 1) * LANES] = bufs["grid", s][at]
         for c in range(2):
-            for h in range(2):
-                s = (c, h)
+            for q in range(QUARTERS):
+                s = (c, q)
                 primal[step] = gather(s, w_copies[s], step + 1, primal[step])
                 if not (last and c == 1):
                     w_copies[s] = back_send(s)
@@ -419,8 +438,8 @@
         copy = remote(totals_a.at[r], totals_a.at[r], sem_n, (e - 1,), lax.rem(r + e, n_region))
         copy.start()
         norm_copies.append(copy)
-    for h in range(2):
-        w_copies[1, h] = back_send((1, h))
+    for q in range(QUARTERS):
+        w_copies[1, q] = back_send((1, q))
     for copy in norm_copies:
         copy.wait()
     totals_b[pl.ds(sub, 1)] = jnp.sum(totals_a[...], axis=0, keepdims=True)
@@ -438,8 +457,8 @@
         copy.wait()
     consensus[...] = cons[...]
     for c in range(2):
-        for h in range(2):
-            for copy in w_copies[c, h]:
+        for q in range(QUARTERS):
+            for copy in w_copies[c, q]:
                 copy.wait_recv()
         update(c, ITERS)
     for copy in norm_copies:
@@ -486,8 +505,7 @@
         pltpu.VMEM((RING - 1, mine, ROWS, LANES), f32),
         pltpu.VMEM((n_pos + 1, ROWS, LANES), f32),
         pltpu.VMEM((RING - 1, nb, ROWS, LANES), f32),
-        pltpu.VMEM((RING - 1, nb, ROWS, LANES), f32),
-        pltpu.VMEM((nb, ROWS, LANES), f32),
+        pltpu.VMEM((RING, nb, ROWS, LANES), f32),
         pltpu.VMEM((RING, nb, ROWS, LANES), f32),
     ]
     state, duals, consensus, norms = pl.pallas_call(
@@ -498,9 +516,10 @@
             pltpu.VMEM((owned, BLOCK, scen), f32),
             pltpu.VMEM((ITERS, 2), f32),
         ),
-        in_specs=[pl.BlockSpec(memory_space=pltpu.HBM)] * 4 + [pl.BlockSpec(memory_space=pltpu.SMEM)],
+        in_specs=[pl.BlockSpec(memory_space=pltpu.HBM)] * 5,
         out_specs=(pl.BlockSpec(memory_space=pltpu.VMEM),) * 4,
         scratch_shapes=[
+            pltpu.SMEM((1, nb), jnp.int32),
             pltpu.VMEM((order, order), jnp.bfloat16),
             pltpu.VMEM((order, scen), jnp.bfloat16),
             pltpu.VMEM((order, scen), f32),
@@ -514,17 +533,17 @@
             pltpu.VMEM((n_region, 8, LANES), f32),
             pltpu.VMEM((n_sub, 8, LANES), f32),
         ]
-        + per_stream * 4
+        + per_stream * (2 * QUARTERS)
         + [
-            dma((6,)),
+            dma((7,)),
             dma((2, 2 * RING - 1)),
             dma((2, 2 * RING - 1)),
-            dma((2, 2, 2, RING - 1)),
-            dma((2, 2, 2, RING - 1)),
-            dma((2, 2, 2, RING - 1)),
-            dma((2, 2, 2, RING - 1)),
-            dma((2, 2, 2, RING - 1)),
-            dma((2, 2, 2, RING - 1)),
+            dma((2, 2, QUARTERS, RING - 1)),
+            dma((2, 2, QUARTERS, RING - 1)),
+            dma((2, 2, QUARTERS, RING - 1)),
+            dma((2, 2, QUARTERS, RING - 1)),
+            dma((2, 2, QUARTERS, RING - 1)),
+            dma((2, 2, QUARTERS, RING - 1)),
             dma((2, n_region - 1 + n_sub - 1)),
         ],
         compiler_params=pltpu.CompilerParams(

time: 98.8 us -> 94.1 us (0.952)
  Pallas kernels: 98.1 us -> 93.3 us
    pallas_call x1, Pallas kernels: 96.1 us -> 91.4 us  [shards(): pl.pallas_call(kernel, out_shape=(pltpu.VMEM((order, scen), f32), pltpu.V...]
where the time goes in v3:
time: 94.1 us; the launch traced here: 94 us
  Pallas kernels  93.3 us (99%)
    pallas_call x1, Pallas kernels, shards(): pl.pallas_call(kernel, out_shape=(pltpu.VMEM((order, scen), f32), pltpu.V...  91.4 us
    pallas_call x1, Pallas kernels, shards(): pl.pallas_call(put_out, out_shape=tuple((jax.ShapeDtypeStruct(a.shape, a....  1.95 us

profile of v3, /device:TPU:1, one launch (start us, length us, event | category | flops | bytes accessed | tf_op | source)
XLA Modules:
  0.0 94.0 jit_solution(735994656521943638)
XLA Ops:
  0.6 91.4 %admm.1 = (f32[2048,256]{1,0:T(8,128)S(1)}, f32[12,128,256]{2,1,0:T(8,128)S(1)}, f32[2,128,256]{2,1,0:T(8,128)S(1)}, f32[2,2]{1,0:T(2,128)S(1)}) custom-call(bf16[2048,2048]{1,0:T(8,128)(2,1)} %kkt_ref.1, bf16[2048,256]{1,0:T(8,128)(2,1)} %cost_ref.1, f32[12,128,256]{2,1,0:T(8,128)} %bitcast.6, f32[2,128,256]{2,1,0:T(8,128)} %bitcast.7, s32[1,12]{1,0:T(1,128)} %target_hbm.1), custom_call_target="tpu_custom_call" | custom-call | tf_op jit(solution)/shard_map/admm/pallas_call | solution.py:511
  92.0 1.9 %put_out.1 = (f32[2048,256]{1,0:T(8,128)}, f32[1536,256]{1,0:T(8,128)}, f32[256,256]{1,0:T(8,128)}, f32[2,2]{1,0:T(2,128)}) custom-call(f32[2048,256]{1,0:T(8,128)S(1)} %get-tuple-element.8.refs_0_, f32[1536,256]{1,0:T(8,128)S(1)} %bitcast.4, f32[256,256]{1,0:T(8,128)S(1)} %bitcast.5, f32[2,2]{1,0:T(2,128)S(1)} %get-tuple-element.11.refs_3_), custom_call_target="tpu_custom_call" | custom-call | tf_op jit(solution)/shard_map/put_out/pallas_call | solution.py:571

commit v4 on v3

--- a/solution.py
+++ b/solution.py
@@ -62,6 +62,9 @@
             src_ref=src, dst_ref=dst, send_sem=sems.at[(0, *index)], recv_sem=sems.at[(1, *index)],
             device_id={"region": region}, device_id_type=MESH,
         )
+
+    def group(ref, sems, index):
+        return remote(ref, ref, sems, index, r)
 
     local = [
         pltpu.make_async_copy(target_hbm, target_ref, sem_local.at[6]),
@@ -119,7 +122,6 @@
     def shard_rows(q, p):
         return pl.ds(pl.multiple_of((q * RING + p) * ROWS, ROWS), ROWS)
 
-    init = {}
     for s in streams:
         c, q = s
         h = q % 2
@@ -127,14 +129,12 @@
             p = ring_add(c1[h], e)
             at = pl.multiple_of(c2[h] * mine + c1[h] * owned, owned)
             src = cons.at[:, shard_rows(q, p), pl.ds(c * LANES, LANES)]
-            init[s, e] = remote(src, bufs["grid", s].at[pl.ds(at, owned)], sem_init, (c, q, e - 1), first(h, e))
-            init[s, e].start()
+            remote(src, bufs["grid", s].at[pl.ds(at, owned)], sem_init, (c,), first(h, e)).start()
     table_copies = []
     for h, e in near:
         i = (RING - 1) * h + e
-        copy = remote(tables.at[0], tables.at[i], sem_table, (i,), first(h, e))
-        copy.start()
-        table_copies.append(copy)
+        remote(tables.at[0], tables.at[i], sem_table, (), first(h, e)).start()
+    table_copies.append(group(tables.at[pl.ds(1, len(near))], sem_table, ()))
     for copy in local[2:]:
         copy.start()
     for s in streams:
@@ -147,20 +147,18 @@
     def send_grid(s):
         c, q = s
         h = q % 2
-        copies = []
         at = pl.ds(pl.multiple_of(c2[h] * mine, mine), mine)
         for e in range(1, RING):
             copy = remote(
-                bufs["grid", s].at[at], bufs["grid", s].at[at], sem_q, (c, q, e - 1), second(h, e)
+                bufs["grid", s].at[at], bufs["grid", s].at[at], sem_q, (c, q), second(h, e)
             )
             copy.start()
-            copies.append(copy)
-        return copies
+        return [group(bufs["grid", s].at[pl.ds(0, (RING - 1) * mine)], sem_q, (c, q))]
 
     q_copies, w_copies, v_copies, p_copies = {}, {}, {}, {}
     for s in streams:
-        for e in range(1, RING):
-            init[s, e].wait()
+        if s[1] == 0:
+            group(cons.at[:, pl.ds(0, (RING - 1) * QUARTERS * ROWS // 2)], sem_init, (s[0],)).wait()
         q_copies[s] = send_grid(s)
 
     for copy in table_copies:
@@ -182,9 +180,8 @@
     count_copies = []
     for h, e in near:
         i = (RING - 1) * h + e
-        copy = remote(partial_v.at[0], partial_v.at[i], sem_count, (i,), first(h, e))
-        copy.start()
-        count_copies.append(copy)
+        remote(partial_v.at[0], partial_v.at[i], sem_count, (), first(h, e)).start()
+    count_copies.append(group(partial_v.at[pl.ds(1, len(near))], sem_count, ()))
     to_scalar.wait()
 
     def table_of(h, e):
@@ -228,40 +225,37 @@
     def back_send(s):
         c, q = s
         h = q % 2
-        copies = []
         for e in (1, 3, 2):
             copy = remote(
-                bufs["back", s].at[e - 1], bufs["fetched", s].at[e], sem_w, (c, q, e - 1), first(h, e)
+                bufs["back", s].at[e - 1], bufs["fetched", s].at[e], sem_w, (c, q), first(h, e)
             )
             copy.start()
-            copies.append(copy)
-        return copies
-
-    def update(c, step):
+        return [group(bufs["back", s], sem_w, (c, q))]
+
+    def update(c, q, step):
         cols = pl.ds(c * LANES, LANES)
 
         def one(slot, total):
             alive = live(slot)
-            for q in range(QUARTERS):
-                for p in range(0, RING, 2):
-                    value = jnp.concatenate(
-                        [bufs["fetched", (c, q)][lax.rem(c1[q % 2] - p - i + RING, RING), slot] for i in range(2)]
-                    )
-                    lo = (q * RING + p) * ROWS
-                    in_block = pl.ds(lo, 2 * ROWS)
-                    old = dual[slot, in_block, cols]
-                    at = pl.ds(pl.multiple_of(slot * BLOCK + lo, 2 * ROWS), 2 * ROWS)
-                    if step > 0:
-                        gap = state[at, cols] - value
-                        if step < ITERS:
-                            total = total + alive * (gap * gap)
-                        old = old + alive * gap
-                        dual[slot, in_block, cols] = old
+            for p in range(0, RING, 2):
+                value = jnp.concatenate(
+                    [bufs["fetched", (c, q)][lax.rem(c1[q % 2] - p - i + RING, RING), slot] for i in range(2)]
+                )
+                lo = (q * RING + p) * ROWS
+                in_block = pl.ds(lo, 2 * ROWS)
+                old = dual[slot, in_block, cols]
+                at = pl.ds(pl.multiple_of(slot * BLOCK + lo, 2 * ROWS), 2 * ROWS)
+                if step > 0:
+                    gap = state[at, cols] - value
                     if step < ITERS:
-                        drive[at, cols] = (penalty * alive * (value - old)).astype(jnp.bfloat16)
+                        total = total + alive * (gap * gap)
+                    old = old + alive * gap
+                    dual[slot, in_block, cols] = old
+                if step < ITERS:
+                    drive[at, cols] = (penalty * alive * (value - old)).astype(jnp.bfloat16)
             return total
 
-        total = lax.fori_loop(0, nb, one, jnp.zeros((2 * ROWS, LANES), jnp.float32))
+        total = lax.fori_loop(0, nb, one, jnp.zeros((2 * ROWS, LANES), jnp.float32), unroll=4)
         return total[:ROWS] + total[ROWS:]
 
     slots_at_once = 4
@@ -272,7 +266,7 @@
         h = q % 2
         return remote(
             bufs["send", s].at[ring_add(c1[h], e), slots], bufs["got", s].at[e - 1, slots],
-            sem_v, (c, q, e - 1), first(h, e),
+            sem_v, (c, q), first(h, e),
         )
 
     def couple_send(c, step):
@@ -301,7 +295,7 @@
 
         lax.fori_loop(0, nb // slots_at_once, one, 0)
         for q in range(QUARTERS):
-            v_copies[c, q] = [sent((c, q), e, pl.ds(0, nb)) for e in (1, 3, 2)]
+            v_copies[c, q] = [group(bufs["got", (c, q)].at[:, pl.ds(0, nb)], sem_v, (c, q))]
 
     def reduce_send(s):
         c, q = s
@@ -323,16 +317,14 @@
             return 0
 
         lax.fori_loop(0, n_pos, one, 0, unroll=8)
-        copies = []
         for e in (1, 3, 2):
             p = ring_add(c2[h], e)
             copy = remote(
                 bufs["psum", s].at[pl.ds(pl.multiple_of(p * mine, mine), mine)], bufs["got2", s].at[e - 1],
-                sem_p, (c, q, e - 1), second(h, e),
+                sem_p, (c, q), second(h, e),
             )
             copy.start()
-            copies.append(copy)
-        p_copies[s] = copies
+        p_copies[s] = [group(bufs["got2", s], sem_p, (c, q))]
 
     def renew_send(s, moved):
         c, q = s
@@ -384,16 +376,15 @@
 
     primal = [zero] * ITERS
     moved = [zero] * ITERS
-    owner_copies = []
     for step in range(ITERS):
         last = step == ITERS - 1
         for c in range(2):
             for q in range(QUARTERS):
                 for copy in w_copies[c, q]:
                     copy.wait_recv()
-            got = update(c, step)
-            if step > 0:
-                primal[step - 1] = primal[step - 1] + got
+                got = update(c, q, step)
+                if step > 0:
+                    primal[step - 1] = primal[step - 1] + got
             couple_send(c, step)
         if last:
             tail = pl.ds(bound, kkt.shape[0] - bound)
@@ -413,10 +404,9 @@
                     copy = remote(
                         bufs["grid", s].at[pl.ds(at, owned)],
                         cons.at[:, shard_rows(q, c1[h]), pl.ds(c * LANES, LANES)],
-                        sem_o, (c, q, e - 1), first(h, e),
+                        sem_o, (), first(h, e),
                     )
                     copy.start()
-                    owner_copies.append(copy)
                 for o in range(owned):
                     at = c2[h] * mine + c1[h] * owned + o
                     cons[o, shard_rows(q, c1[h]), c * LANES : (c + 1) * LANES] = bufs["grid", s][at]
@@ -432,38 +422,37 @@
         tile = jnp.where(row == 2 * step, jnp.sum(primal[step], axis=0, keepdims=True), tile)
         change = (penalty * penalty) * jnp.sum(moved[step], axis=0, keepdims=True)
         tile = jnp.where(row == 2 * step + 1, change, tile)
-    totals_a[pl.ds(r, 1)] = tile[None]
-    norm_copies = []
-    for e in range(1, n_region):
-        copy = remote(totals_a.at[r], totals_a.at[r], sem_n, (e - 1,), lax.rem(r + e, n_region))
-        copy.start()
-        norm_copies.append(copy)
-    for q in range(QUARTERS):
-        w_copies[1, q] = back_send((1, q))
-    for copy in norm_copies:
-        copy.wait()
-    totals_b[pl.ds(sub, 1)] = jnp.sum(totals_a[...], axis=0, keepdims=True)
+    totals_b[pl.ds(sub, 1)] = tile[None]
     norm_copies = []
     for e in range(1, n_sub):
         copy = pltpu.make_async_remote_copy(
             src_ref=totals_b.at[sub], dst_ref=totals_b.at[sub],
-            send_sem=sem_n.at[0, n_region - 2 + e], recv_sem=sem_n.at[1, n_region - 2 + e],
+            send_sem=sem_n.at[0, 1], recv_sem=sem_n.at[1, 1],
             device_id={"sub": lax.rem(sub + e, n_sub)}, device_id_type=MESH,
         )
         copy.start()
-        norm_copies.append(copy)
-
-    for copy in owner_copies:
+    norm_copies.append(group(totals_b.at[pl.ds(0, n_sub - 1)], sem_n, (1,)))
+    for q in range(QUARTERS - 1):
+        w_copies[1, q] = back_send((1, q))
+    for copy in norm_copies:
         copy.wait()
+    totals_a[pl.ds(r, 1)] = jnp.sum(totals_b[...], axis=0, keepdims=True)
+    norm_copies = []
+    for e in range(1, n_region):
+        remote(totals_a.at[r], totals_a.at[r], sem_n, (0,), lax.rem(r + e, n_region)).start()
+    norm_copies.append(group(totals_a.at[pl.ds(0, n_region - 1)], sem_n, (0,)))
+    w_copies[1, QUARTERS - 1] = back_send((1, QUARTERS - 1))
+
+    group(cons.at[:, pl.ds(0, (RING - 1) * QUARTERS * ROWS)], sem_o, ()).wait()
     consensus[...] = cons[...]
     for c in range(2):
         for q in range(QUARTERS):
             for copy in w_copies[c, q]:
                 copy.wait_recv()
-        update(c, ITERS)
+            update(c, q, ITERS)
     for copy in norm_copies:
         copy.wait()
-    table = jnp.sum(jnp.sum(totals_b[...], axis=0), axis=1, keepdims=True)
+    table = jnp.sum(jnp.sum(totals_a[...], axis=0), axis=1, keepdims=True)
     scale = 1.0 / (n_region * n_sub * 2 * LANES * BLOCK)
     table = jnp.sqrt(table * scale)
     small = (ITERS, 2)
@@ -536,15 +525,15 @@
         + per_stream * (2 * QUARTERS)
         + [
             dma((7,)),
-            dma((2, 2 * RING - 1)),
-            dma((2, 2 * RING - 1)),
-            dma((2, 2, QUARTERS, RING - 1)),
-            dma((2, 2, QUARTERS, RING - 1)),
-            dma((2, 2, QUARTERS, RING - 1)),
-            dma((2, 2, QUARTERS, RING - 1)),
-            dma((2, 2, QUARTERS, RING - 1)),
-            dma((2, 2, QUARTERS, RING - 1)),
-            dma((2, n_region - 1 + n_sub - 1)),
+            dma((2,)),
+            dma((2,)),
+            dma((2, 2)),
+            dma((2, 2, QUARTERS)),
+            dma((2, 2, QUARTERS)),
+            dma((2, 2, QUARTERS)),
+            dma((2, 2, QUARTERS)),
+            dma((2,)),
+            dma((2, 2)),
         ],
         compiler_params=pltpu.CompilerParams(
             collective_id=0, has_side_effects=True, vmem_limit_bytes=40 * 2**20

time: 94.1 us -> 91.4 us (0.971)
  Pallas kernels: 93.3 us -> 90.7 us
    pallas_call x1, Pallas kernels: 91.4 us -> 88.7 us  [shards(): pl.pallas_call(kernel, out_shape=(pltpu.VMEM((order, scen), f32), pltpu.V...]
where the time goes in v4:
time: 91.4 us; the launch traced here: 91.3 us
  Pallas kernels  90.7 us (99%)
    pallas_call x1, Pallas kernels, shards(): pl.pallas_call(kernel, out_shape=(pltpu.VMEM((order, scen), f32), pltpu.V...  88.7 us
    pallas_call x1, Pallas kernels, shards(): pl.pallas_call(put_out, out_shape=tuple((jax.ShapeDtypeStruct(a.shape, a....  1.95 us

profile of v4, /device:TPU:1, one launch (start us, length us, event | category | flops | bytes accessed | tf_op | source)
XLA Modules:
  0.0 91.3 jit_solution(12547221889147674324)
XLA Ops:
  0.6 88.7 %admm.1 = (f32[2048,256]{1,0:T(8,128)S(1)}, f32[12,128,256]{2,1,0:T(8,128)S(1)}, f32[2,128,256]{2,1,0:T(8,128)S(1)}, f32[2,2]{1,0:T(2,128)S(1)}) custom-call(bf16[2048,2048]{1,0:T(8,128)(2,1)} %kkt_ref.1, bf16[2048,256]{1,0:T(8,128)(2,1)} %cost_ref.1, f32[12,128,256]{2,1,0:T(8,128)} %bitcast.6, f32[2,128,256]{2,1,0:T(8,128)} %bitcast.7, s32[1,12]{1,0:T(1,128)} %target_hbm.1), custom_call_target="tpu_custom_call" | custom-call | tf_op jit(solution)/shard_map/admm/pallas_call | solution.py:500
  89.4 1.9 %put_out.1 = (f32[2048,256]{1,0:T(8,128)}, f32[1536,256]{1,0:T(8,128)}, f32[256,256]{1,0:T(8,128)}, f32[2,2]{1,0:T(2,128)}) custom-call(f32[2048,256]{1,0:T(8,128)S(1)} %get-tuple-element.8.refs_0_, f32[1536,256]{1,0:T(8,128)S(1)} %bitcast.4, f32[256,256]{1,0:T(8,128)S(1)} %bitcast.5, f32[2,2]{1,0:T(2,128)S(1)} %get-tuple-element.11.refs_3_), custom_call_target="tpu_custom_call" | custom-call | tf_op jit(solution)/shard_map/put_out/pallas_call | solution.py:560

commit v5 on v4

--- a/solution.py
+++ b/solution.py
@@ -36,7 +36,7 @@
     bound = nb * BLOCK
     streams = [(c, q) for c in range(2) for q in range(QUARTERS)]
     bufs = {}
-    names = ("send", "got", "psum", "got2", "grid", "back", "fetched", "held")
+    names = ("send", "got", "psum", "got2", "grid", "back", "fetched")
     rest = list(rest)
     for s in streams:
         for name in names:
@@ -190,7 +190,7 @@
     def live(s):
         return jnp.where(target_ref[0, s] >= 0, 1.0, 0.0).astype(jnp.float32)
 
-    def gather(s, before, step, primal):
+    def gather(s, before):
         c, q = s
         h = q % 2
         for copy in q_copies[s]:
@@ -199,28 +199,17 @@
             copy.wait_send()
         grid = bufs["grid", s]
         for e in (1, 3, 2, 0):
-            back = 0 if e == 0 else RING - e
-            t = table_of(h, back)
-
-            def one(slot, primal):
-                place = table_s[t, 4 + h, slot]
-                value = grid[place]
+            t = table_of(h, 0 if e == 0 else RING - e)
+
+            def one(slot, _):
+                value = grid[table_s[t, 4 + h, slot]]
                 if e:
                     bufs["back", s][e - 1, slot] = value
                 else:
                     bufs["fetched", s][0, slot] = value
-                if step:
-                    sent = bufs["got", s][back - 1, slot] if e else bufs["send", s][c1[h], slot]
-                    if step == 1:
-                        bufs["held", s][e, slot] = sent - value
-                    else:
-                        alive = jnp.where(place < n_pos, 1.0, 0.0).astype(jnp.float32)
-                        gap = sent - bufs["held", s][e, slot] - value
-                        primal = primal + alive * (gap * gap)
-                return primal
-
-            primal = lax.fori_loop(0, nb, one, primal, unroll=4)
-        return primal
+                return 0
+
+            lax.fori_loop(0, nb, one, 0, unroll=4)
 
     def back_send(s):
         c, q = s
@@ -275,7 +264,7 @@
             for copy in v_copies.get((c, q), ()):
                 copy.wait_send()
 
-        def one(i, _):
+        def one(i, total):
             at = pl.ds(pl.multiple_of(i * chunk, chunk), chunk)
             rows = base[at, cols] + jnp.dot(
                 kkt[at, 0:bound], drive[:, cols], preferred_element_type=jnp.float32
@@ -288,14 +277,19 @@
                     for p in range(RING):
                         lo = (q * RING + p) * ROWS
                         bufs["send", (c, q)][p, slot] = v[lo : lo + ROWS]
+                        if step == ITERS - 1:
+                            before = bufs["fetched", (c, q)][lax.rem(c1[q % 2] - p + RING, RING), slot]
+                            drift = rows[j * BLOCK + lo : j * BLOCK + lo + ROWS] - before
+                            total = total + live(slot) * (drift * drift)
             for q in range(QUARTERS):
                 for e in (1, 3, 2):
                     sent((c, q), e, pl.ds(i * slots_at_once, slots_at_once)).start()
-            return 0
-
-        lax.fori_loop(0, nb // slots_at_once, one, 0)
+            return total
+
+        total = lax.fori_loop(0, nb // slots_at_once, one, zero)
         for q in range(QUARTERS):
             v_copies[c, q] = [group(bufs["got", (c, q)].at[:, pl.ds(0, nb)], sem_v, (c, q))]
+        return total
 
     def reduce_send(s):
         c, q = s
@@ -347,7 +341,7 @@
         return moved
 
     for s in streams:
-        gather(s, (), 0, zero)
+        gather(s, ())
         w_copies[s] = back_send(s)
     local[2].wait()
     local[4].wait()
@@ -385,7 +379,7 @@
                 got = update(c, q, step)
                 if step > 0:
                     primal[step - 1] = primal[step - 1] + got
-            couple_send(c, step)
+            primal[step] = primal[step] + couple_send(c, step)
         if last:
             tail = pl.ds(bound, kkt.shape[0] - bound)
             state[tail] = base[tail] + jnp.dot(
@@ -410,38 +404,30 @@
                 for o in range(owned):
                     at = c2[h] * mine + c1[h] * owned + o
                     cons[o, shard_rows(q, c1[h]), c * LANES : (c + 1) * LANES] = bufs["grid", s][at]
-        for c in range(2):
-            for q in range(QUARTERS):
-                s = (c, q)
-                primal[step] = gather(s, w_copies[s], step + 1, primal[step])
-                if not (last and c == 1):
-                    w_copies[s] = back_send(s)
+        if not last:
+            for s in streams:
+                gather(s, w_copies[s])
+                w_copies[s] = back_send(s)
 
     tile = jnp.zeros((8, LANES), jnp.float32)
     for step in range(ITERS):
         tile = jnp.where(row == 2 * step, jnp.sum(primal[step], axis=0, keepdims=True), tile)
-        change = (penalty * penalty) * jnp.sum(moved[step], axis=0, keepdims=True)
-        tile = jnp.where(row == 2 * step + 1, change, tile)
+        tile = jnp.where(row == 2 * step + 1, jnp.sum(moved[step], axis=0, keepdims=True), tile)
     totals_b[pl.ds(sub, 1)] = tile[None]
-    norm_copies = []
     for e in range(1, n_sub):
-        copy = pltpu.make_async_remote_copy(
+        pltpu.make_async_remote_copy(
             src_ref=totals_b.at[sub], dst_ref=totals_b.at[sub],
             send_sem=sem_n.at[0, 1], recv_sem=sem_n.at[1, 1],
             device_id={"sub": lax.rem(sub + e, n_sub)}, device_id_type=MESH,
-        )
-        copy.start()
-    norm_copies.append(group(totals_b.at[pl.ds(0, n_sub - 1)], sem_n, (1,)))
-    for q in range(QUARTERS - 1):
-        w_copies[1, q] = back_send((1, q))
-    for copy in norm_copies:
-        copy.wait()
-    totals_a[pl.ds(r, 1)] = jnp.sum(totals_b[...], axis=0, keepdims=True)
-    norm_copies = []
-    for e in range(1, n_region):
-        remote(totals_a.at[r], totals_a.at[r], sem_n, (0,), lax.rem(r + e, n_region)).start()
-    norm_copies.append(group(totals_a.at[pl.ds(0, n_region - 1)], sem_n, (0,)))
-    w_copies[1, QUARTERS - 1] = back_send((1, QUARTERS - 1))
+        ).start()
+    for s in streams:
+        if s == (1, 0):
+            group(totals_b.at[pl.ds(0, n_sub - 1)], sem_n, (1,)).wait()
+            totals_a[pl.ds(r, 1)] = jnp.sum(totals_b[...], axis=0, keepdims=True)
+            for e in range(1, n_region):
+                remote(totals_a.at[r], totals_a.at[r], sem_n, (0,), lax.rem(r + e, n_region)).start()
+        gather(s, w_copies[s])
+        w_copies[s] = back_send(s)
 
     group(cons.at[:, pl.ds(0, (RING - 1) * QUARTERS * ROWS)], sem_o, ()).wait()
     consensus[...] = cons[...]
@@ -450,10 +436,14 @@
             for copy in w_copies[c, q]:
                 copy.wait_recv()
             update(c, q, ITERS)
-    for copy in norm_copies:
-        copy.wait()
+    group(totals_a.at[pl.ds(0, n_region - 1)], sem_n, (0,)).wait()
     table = jnp.sum(jnp.sum(totals_a[...], axis=0), axis=1, keepdims=True)
     scale = 1.0 / (n_region * n_sub * 2 * LANES * BLOCK)
+    final = 2 * (ITERS - 1)
+    rest = table[final : final + 1] - table[final + 1 : final + 2]
+    rank = lax.broadcasted_iota(jnp.int32, table.shape, 0)
+    table = jnp.where(rank == final, jnp.maximum(rest, 0.0), table)
+    table = jnp.where(lax.rem(rank, 2) == 1, (penalty * penalty) * table, table)
     table = jnp.sqrt(table * scale)
     small = (ITERS, 2)
     which = lax.broadcasted_iota(jnp.int32, small, 0) * 2 + lax.broadcasted_iota(jnp.int32, small, 1)
@@ -494,7 +484,6 @@
         pltpu.VMEM((RING - 1, mine, ROWS, LANES), f32),
         pltpu.VMEM((n_pos + 1, ROWS, LANES), f32),
         pltpu.VMEM((RING - 1, nb, ROWS, LANES), f32),
-        pltpu.VMEM((RING, nb, ROWS, LANES), f32),
         pltpu.VMEM((RING, nb, ROWS, LANES), f32),
     ]
     state, duals, consensus, norms = pl.pallas_call(

time: 91.4 us -> 88.8 us (0.972); the launches traced: 91.3 us -> 87.4 us
  Pallas kernels: 90.7 us -> 86.8 us
    pallas_call x1, Pallas kernels: 88.7 us -> 84.8 us  [shards(): pl.pallas_call(kernel, out_shape=(pltpu.VMEM((order, scen), f32), pltpu.V...]
where the time goes in v5:
time: 88.8 us; the launch traced here: 87.4 us
  Pallas kernels  86.8 us (98%)
    pallas_call x1, Pallas kernels, shards(): pl.pallas_call(kernel, out_shape=(pltpu.VMEM((order, scen), f32), pltpu.V...  84.8 us
    pallas_call x1, Pallas kernels, shards(): pl.pallas_call(put_out, out_shape=tuple((jax.ShapeDtypeStruct(a.shape, a....  1.95 us

profile of v5, /device:TPU:1, one launch (start us, length us, event | category | flops | bytes accessed | tf_op | source)
XLA Modules:
  0.0 87.4 jit_solution(2251032375151631553)
XLA Ops:
  0.6 84.8 %admm.1 = (f32[2048,256]{1,0:T(8,128)S(1)}, f32[12,128,256]{2,1,0:T(8,128)S(1)}, f32[2,128,256]{2,1,0:T(8,128)S(1)}, f32[2,2]{1,0:T(2,128)S(1)}) custom-call(bf16[2048,2048]{1,0:T(8,128)(2,1)} %kkt_ref.1, bf16[2048,256]{1,0:T(8,128)(2,1)} %cost_ref.1, f32[12,128,256]{2,1,0:T(8,128)} %bitcast.6, f32[2,128,256]{2,1,0:T(8,128)} %bitcast.7, s32[1,12]{1,0:T(1,128)} %target_hbm.1), custom_call_target="tpu_custom_call" | custom-call | tf_op jit(solution)/shard_map/admm/pallas_call | solution.py:489
  85.5 1.9 %put_out.1 = (f32[2048,256]{1,0:T(8,128)}, f32[1536,256]{1,0:T(8,128)}, f32[256,256]{1,0:T(8,128)}, f32[2,2]{1,0:T(2,128)}) custom-call(f32[2048,256]{1,0:T(8,128)S(1)} %get-tuple-element.8.refs_0_, f32[1536,256]{1,0:T(8,128)S(1)} %bitcast.4, f32[256,256]{1,0:T(8,128)S(1)} %bitcast.5, f32[2,2]{1,0:T(2,128)S(1)} %get-tuple-element.11.refs_3_), custom_call_target="tpu_custom_call" | custom-call | tf_op jit(solution)/shard_map/put_out/pallas_call | solution.py:549

commit v6 on v5

--- a/solution.py
+++ b/solution.py
@@ -392,15 +392,6 @@
             if last:
                 c, q = s
                 h = q % 2
-                for e in range(1, RING):
-                    p = ring_add(c1[h], e)
-                    at = pl.multiple_of(c2[h] * mine + p * owned, owned)
-                    copy = remote(
-                        bufs["grid", s].at[pl.ds(at, owned)],
-                        cons.at[:, shard_rows(q, c1[h]), pl.ds(c * LANES, LANES)],
-                        sem_o, (), first(h, e),
-                    )
-                    copy.start()
                 for o in range(owned):
                     at = c2[h] * mine + c1[h] * owned + o
                     cons[o, shard_rows(q, c1[h]), c * LANES : (c + 1) * LANES] = bufs["grid", s][at]
@@ -429,13 +420,25 @@
         gather(s, w_copies[s])
         w_copies[s] = back_send(s)
 
-    group(cons.at[:, pl.ds(0, (RING - 1) * QUARTERS * ROWS)], sem_o, ()).wait()
-    consensus[...] = cons[...]
+    for s in streams:
+        c, q = s
+        h = q % 2
+        for e in range(1, RING):
+            p = ring_add(c1[h], e)
+            at = pl.multiple_of(c2[h] * mine + p * owned, owned)
+            copy = remote(
+                bufs["grid", s].at[pl.ds(at, owned)],
+                cons.at[:, shard_rows(q, c1[h]), pl.ds(c * LANES, LANES)],
+                sem_o, (), first(h, e),
+            )
+            copy.start()
     for c in range(2):
         for q in range(QUARTERS):
             for copy in w_copies[c, q]:
                 copy.wait_recv()
             update(c, q, ITERS)
+    group(cons.at[:, pl.ds(0, (RING - 1) * QUARTERS * ROWS)], sem_o, ()).wait()
+    consensus[...] = cons[...]
     group(totals_a.at[pl.ds(0, n_region - 1)], sem_n, (0,)).wait()
     table = jnp.sum(jnp.sum(totals_a[...], axis=0), axis=1, keepdims=True)
     scale = 1.0 / (n_region * n_sub * 2 * LANES * BLOCK)

time: 88.8 us -> 88.8 us (level); the launches traced: 87.4 us -> 88.3 us
  Pallas kernels: 86.8 us -> 87.7 us
    pallas_call x1, Pallas kernels: 84.8 us -> 85.8 us  [shards(): pl.pallas_call(kernel, out_shape=(pltpu.VMEM((order, scen), f32), pltpu.V...]
where the time goes in v6:
time: 88.8 us; the launch traced here: 88.3 us
  Pallas kernels  87.7 us (99%)
    pallas_call x1, Pallas kernels, shards(): pl.pallas_call(kernel, out_shape=(pltpu.VMEM((order, scen), f32), pltpu.V...  85.8 us
    pallas_call x1, Pallas kernels, shards(): pl.pallas_call(put_out, out_shape=tuple((jax.ShapeDtypeStruct(a.shape, a....  1.95 us

profile of v6, /device:TPU:1, one launch (start us, length us, event | category | flops | bytes accessed | tf_op | source)
XLA Modules:
  0.0 88.3 jit_solution(6498960457981385298)
XLA Ops:
  0.6 85.8 %admm.1 = (f32[2048,256]{1,0:T(8,128)S(1)}, f32[12,128,256]{2,1,0:T(8,128)S(1)}, f32[2,128,256]{2,1,0:T(8,128)S(1)}, f32[2,2]{1,0:T(2,128)S(1)}) custom-call(bf16[2048,2048]{1,0:T(8,128)(2,1)} %kkt_ref.1, bf16[2048,256]{1,0:T(8,128)(2,1)} %cost_ref.1, f32[12,128,256]{2,1,0:T(8,128)} %bitcast.6, f32[2,128,256]{2,1,0:T(8,128)} %bitcast.7, s32[1,12]{1,0:T(1,128)} %target_hbm.1), custom_call_target="tpu_custom_call" | custom-call | tf_op jit(solution)/shard_map/admm/pallas_call | solution.py:492
  86.4 1.9 %put_out.1 = (f32[2048,256]{1,0:T(8,128)}, f32[1536,256]{1,0:T(8,128)}, f32[256,256]{1,0:T(8,128)}, f32[2,2]{1,0:T(2,128)}) custom-call(f32[2048,256]{1,0:T(8,128)S(1)} %get-tuple-element.8.refs_0_, f32[1536,256]{1,0:T(8,128)S(1)} %bitcast.4, f32[256,256]{1,0:T(8,128)S(1)} %bitcast.5, f32[2,2]{1,0:T(2,128)S(1)} %get-tuple-element.11.refs_3_), custom_call_target="tpu_custom_call" | custom-call | tf_op jit(solution)/shard_map/put_out/pallas_call | solution.py:552
